TPU v7x, 128 devices: a whole 4x4x4 slice. The times are simulated.
128 devices in a mesh: ctx: 16 (over y_hi, x, core), head: 8 (over z, y_lo).
Axes of the slice: x: 4, y: 4 (y_hi: 2, y_lo: 2; y = y_hi * 2 + y_lo), z: 4, core: 2. Of those that a mesh axis runs over, the one named last changes fastest.
Arguments:
- queries: bfloat16 [4096, 4096], P('ctx', 'head'), may hold values from -80 to 80
- keys: bfloat16 [4096, 2048], P('ctx', 'head'), may hold values from -6 to 6
- values: bfloat16 [4096, 2048], P('ctx', 'head'), may hold values from -6 to 6
- grad_out: bfloat16 [4096, 4096], P('ctx', 'head'), may hold values from -6 to 6
- chosen: int32 [64, 16, 16], P('ctx', 'head'), may hold values from 0 to 63, as said below
- w_query: bfloat16 [4608, 4096], P(None, 'head'), may hold values from -0.09375 to 0.09375
- w_key: bfloat16 [4608, 2048], P(None, 'head'), may hold values from -0.09375 to 0.09375
- w_value: bfloat16 [4608, 2048], P(None, 'head'), may hold values from -0.09375 to 0.09375
Outputs:
- grad_queries: bfloat16 [4096, 4096], P('ctx', 'head')
- grad_keys: bfloat16 [4096, 2048], P('ctx', 'head')
- grad_values: bfloat16 [4096, 2048], P('ctx', 'head')
- grad_input: bfloat16 [4096, 4608], P('ctx', 'head')
Inputs may be any that keep to these rules, and one draw needn't show every extreme that they name: `chosen`: each list names 16 different blocks; it always names block 0 and the query's own block, and a query block b below 16 names every block 0 .. b; entries above the query's own block contribute no keys.
All inputs are finite; a program needn't handle non-finite values.
Results may differ from a plain program's by a relative error of at most 0.019.
Values may be sent and summed in bfloat16 or wider, within the bound.
A program may use at most 128 MiB of HBM per device.

v0:
```python
import math

import jax
import jax.numpy as jnp
from jax import lax
from jax.sharding import PartitionSpec as P

HEAD_DIM = 128
BLOCK = 64


def block_grads(key_blocks, value_blocks, query_block, grad_block, picked, first_row):
    block_len = query_block.shape[0]
    head_dim = key_blocks.shape[2]
    heads_per = query_block.shape[1] // head_dim
    scaling = 1.0 / math.sqrt(head_dim)
    key_rows = (
        picked[:, None] * block_len + jnp.arange(block_len, dtype=jnp.int32)[None, :]
    ).reshape(-1)
    chosen_keys = jnp.take(key_blocks, picked, axis=0).reshape(-1, head_dim)
    chosen_values = jnp.take(value_blocks, picked, axis=0).reshape(-1, head_dim)
    query_rows = query_block.reshape(block_len * heads_per, head_dim)
    grad_rows = grad_block.reshape(block_len * heads_per, head_dim)
    positions = first_row + jnp.repeat(jnp.arange(block_len, dtype=jnp.int32), heads_per)
    allowed = key_rows[None, :] <= positions[:, None]
    contract = (((1,), (1,)), ((), ()))
    across = (((0,), (0,)), ((), ()))
    scores = scaling * lax.dot_general(
        query_rows, chosen_keys, contract, preferred_element_type=jnp.float32
    )
    scores = jnp.where(allowed, scores, -1e30)
    row_max = jnp.max(scores, axis=1, keepdims=True)
    weights = jnp.where(allowed, jnp.exp(scores - row_max), 0.0)
    weights = weights / jnp.sum(weights, axis=1, keepdims=True)
    weights_low = weights.astype(jnp.bfloat16)
    attended = jnp.dot(weights_low, chosen_values, preferred_element_type=jnp.float32)
    deltas = jnp.sum(grad_rows.astype(jnp.float32) * attended, axis=1, keepdims=True)
    grad_weights = lax.dot_general(
        grad_rows, chosen_values, contract, preferred_element_type=jnp.float32
    )
    grad_scores = (weights * (grad_weights - deltas)).astype(jnp.bfloat16)
    grad_query = scaling * jnp.dot(grad_scores, chosen_keys, preferred_element_type=jnp.float32)
    grad_key = scaling * lax.dot_general(
        grad_scores, query_rows, across, preferred_element_type=jnp.float32
    )
    grad_value = lax.dot_general(weights_low, grad_rows, across, preferred_element_type=jnp.float32)
    grad_query = grad_query.astype(jnp.bfloat16).reshape(block_len, heads_per * head_dim)
    grad_key = grad_key.reshape(picked.shape[0], block_len * head_dim)
    grad_value = grad_value.reshape(picked.shape[0], block_len * head_dim)
    return (grad_query, grad_key, grad_value)


def group_pass(key_all, value_all, query_part, grad_part, picked, first_block):
    head_dim = key_all.shape[1]
    total_rows = key_all.shape[0]
    block_count = total_rows // BLOCK
    key_blocks = key_all.reshape(block_count, BLOCK, head_dim)
    value_blocks = value_all.reshape(block_count, BLOCK, head_dim)
    heads_per = query_part.shape[1] // head_dim
    blocks_here = query_part.shape[0] // BLOCK
    block_step = math.gcd(blocks_here, max(1, 512 // (BLOCK * heads_per)))
    turns = blocks_here // block_step
    queries_in = query_part.reshape(turns, block_step, BLOCK, query_part.shape[1])
    grads_in = grad_part.reshape(turns, block_step, BLOCK, grad_part.shape[1])
    picked_in = picked.reshape(turns, block_step, picked.shape[1])
    first_rows = ((first_block + jnp.arange(blocks_here, dtype=jnp.int32)) * BLOCK).reshape(
        turns, block_step
    )
    mapped = jax.vmap(block_grads, in_axes=(None, None, 0, 0, 0, 0))

    def update_step(running, inputs):
        query_set, grad_set, picked_set, row_set = inputs
        grad_q, grad_k, grad_v = mapped(
            key_blocks, value_blocks, query_set, grad_set, picked_set, row_set
        )
        flat_blocks = picked_set.reshape(-1)
        total_k = running[0].at[flat_blocks].add(grad_k.reshape(-1, BLOCK * head_dim))
        total_v = running[1].at[flat_blocks].add(grad_v.reshape(-1, BLOCK * head_dim))
        return ((total_k, total_v), grad_q)

    zeros_acc = jnp.zeros((block_count, BLOCK * head_dim), jnp.float32)
    (accum_k, accum_v), grad_q = lax.scan(
        update_step, (zeros_acc, zeros_acc), (queries_in, grads_in, picked_in, first_rows)
    )
    return (
        grad_q.reshape(query_part.shape),
        accum_k.reshape(total_rows, head_dim),
        accum_v.reshape(total_rows, head_dim),
    )


def body(queries, keys, values, grad_out, chosen, w_query, w_key, w_value):
    head_dim = HEAD_DIM
    groups_here = keys.shape[1] // head_dim
    query_width = queries.shape[1] // groups_here
    blocks_here = queries.shape[0] // BLOCK
    first_block = lax.axis_index("ctx") * blocks_here
    query_grads = []
    key_all, value_all = (
        lax.all_gather(keys, "ctx", axis=0, tiled=True),
        lax.all_gather(values, "ctx", axis=0, tiled=True),
    )
    parts_k = []
    parts_v = []
    for group_index in range(groups_here):
        key_cols = slice(group_index * head_dim, (group_index + 1) * head_dim)
        query_cols = slice(group_index * query_width, (group_index + 1) * query_width)
        grad_q, group_k, group_v = group_pass(
            key_all[:, key_cols],
            value_all[:, key_cols],
            queries[:, query_cols],
            grad_out[:, query_cols],
            chosen[:, group_index, :],
            first_block,
        )
        query_grads.append(grad_q)
        parts_k.append(group_k)
        parts_v.append(group_v)
    accum_k = jnp.concatenate(parts_k, axis=1)
    accum_v = jnp.concatenate(parts_v, axis=1)
    sums_k, sums_v = (
        lax.psum_scatter(
            accum_k.astype(jnp.bfloat16), "ctx", scatter_dimension=0, tiled=True
        ).astype(jnp.float32),
        lax.psum_scatter(
            accum_v.astype(jnp.bfloat16), "ctx", scatter_dimension=0, tiled=True
        ).astype(jnp.float32),
    )
    grad_queries = jnp.concatenate(query_grads, axis=1)
    grad_keys = sums_k.astype(jnp.bfloat16)
    grad_values = sums_v.astype(jnp.bfloat16)
    contract = (((1,), (1,)), ((), ()))
    partial_input = lax.dot_general(
        grad_queries, w_query, contract, preferred_element_type=jnp.float32
    )
    partial_input = partial_input + lax.dot_general(
        grad_keys, w_key, contract, preferred_element_type=jnp.float32
    )
    partial_input = partial_input + lax.dot_general(
        grad_values, w_value, contract, preferred_element_type=jnp.float32
    )
    grad_input = lax.psum_scatter(
        partial_input.astype(jnp.bfloat16), "head", scatter_dimension=1, tiled=True
    )
    return (grad_queries, grad_keys, grad_values, grad_input)


def solution(mesh):
    return jax.shard_map(
        body,
        mesh=mesh,
        in_specs=(
            P("ctx", "head"),
            P("ctx", "head"),
            P("ctx", "head"),
            P("ctx", "head"),
            P("ctx", "head", None),
            P(None, "head"),
            P(None, "head"),
            P(None, "head"),
        ),
        out_specs=(P("ctx", "head"), P("ctx", "head"), P("ctx", "head"), P("ctx", "head")),
        check_vma=False,
    )
```

profile of v0, /device:TPU:0, one launch (start us, length us, event | category | flops | bytes accessed | tf_op | source)
XLA Modules:
  0.0 389.2 jit_solution(11638567934295345563)
XLA Ops:
  10.4 1.0 fusion.47
  12.2 1.0 fusion.48
  18.1 43.0 %all-gather.5.cloned.1.call-done = bf16[4096,256]{1,0:T(8,128)(2,1)} async-done(((bf16[256,256]{1,0:T(8,128)(2,1)}), bf16[4096,256]{1,0:T(8,128)(2,1)}) %all-gather.5.cloned.1.call-update) | async-done | bytes 2097168 | tf_op jit(solution)/shard_map/all_gather | solution.py:101
  61.1 3.0 fusion.46
  64.1 2.0 gather_fusion.3
  66.1 44.6 %all-gather.3.cloned.1.call-done = bf16[4096,256]{1,0:T(8,128)(2,1)} async-done(((bf16[256,256]{1,0:T(8,128)(2,1)}), bf16[4096,256]{1,0:T(8,128)(2,1)}) %all-gather.3.cloned.1.call-update) | async-done | bytes 2097168 | tf_op jit(solution)/shard_map/all_gather | solution.py:100
  110.7 3.1 fusion.45
  113.8 2.9 gather_fusion.2
  116.7 2.9 gather_fusion.1
  119.6 2.9 gather_fusion
  122.4 3.2 broadcast_select_fusion.3
  125.6 4.1 %fusion.49 = (f32[4,128]{1,0:T(4,128)}, f32[4,128,1024]{1,2,0:T(8,128)}) fusion(s32[4,128]{1,0:T(4,128)} %broadcast_add_fusion.2, s32[4,1024]{1,0:T(4,128)S(1)} %copy-done.13, bf16[4,1024,128]{2,1,0:T(8,128)(2,1)} %bitcast.70, bf16[4,128,128]{2,1,0:T(8,128)(2,1)} %reshape.278), kind=kOutput, calls=%fused_computation.91 | convolution fusion | flops 137888768 | bytes 3297280 | tf_op jit(solution)/shard_map/while/body/eval_jaxpr/vmap()/sub | solution.py:33
  129.7 2.6 fusion.9
  133.1 1.0 copy-done.2
  134.1 1.7 convolution_multiply_fusion.1
  135.8 2.8 reshape.336
  138.6 5.4 %scatter_custom_fusion = f32[64,8192]{1,0:T(8,128)} fusion(s32[64]{0:T(128)} %fusion.33, f32[64,8192]{1,0:T(8,128)} %reshape.336, f32[]{:T(128)} %constant.58.clone.1), kind=kCustom, calls=%fused_computation.41 | custom fusion | flops 524288 | bytes 2097664 | tf_op jit(solution)/shard_map/while/body/eval_jaxpr/scatter-add | solution.py:77
  144.1 2.7 convert.16
  146.8 2.3 reshape.292
  149.1 2.9 broadcast_select_fusion.1
  151.9 4.1 %fusion.50 = (f32[4,128]{1,0:T(4,128)}, f32[4,128,1024]{1,2,0:T(8,128)}) fusion(s32[4,1024]{1,0:T(4,128)S(1)} %copy-done.12, s32[4,128]{1,0:T(4,128)} %broadcast_add_fusion.2, bf16[4,1024,128]{2,1,0:T(8,128)(2,1)} %bitcast.72, bf16[4,128,128]{2,1,0:T(8,128)(2,1)S(1)} %reshape.285), kind=kOutput, calls=%fused_computation.92 | convolution fusion | flops 137888768 | bytes 3297280 | tf_op jit(solution)/shard_map/while/body/eval_jaxpr/vmap()/sub | solution.py:33
  156.0 2.3 fusion.10
  159.9 1.8 convolution_multiply_fusion
  161.7 2.8 reshape.344
  164.5 5.5 %scatter_custom_fusion.1 = f32[64,8192]{1,0:T(8,128)} fusion(s32[64]{0:T(128)} %fusion.34, f32[64,8192]{1,0:T(8,128)} %reshape.344, f32[]{:T(128)} %constant.58.clone.1), kind=kCustom, calls=%fused_computation.39 | custom fusion | flops 524288 | bytes 2097664 | tf_op jit(solution)/shard_map/while/body/eval_jaxpr/scatter-add | solution.py:77
  170.0 1.7 convert.17
  171.7 1.3 reshape.295
  173.0 3.1 pad_maximum_fusion
  177.0 3.3 fusion.42
  180.4 2.7 reshape.352
  183.1 5.5 %scatter_custom_fusion.2 = f32[64,8192]{1,0:T(8,128)} fusion(s32[64]{0:T(128)} %fusion.33, f32[64,8192]{1,0:T(8,128)} %reshape.352, f32[]{:T(128)} %constant.58.clone.1), kind=kCustom, calls=%fused_computation.37 | custom fusion | flops 524288 | bytes 2097664 | tf_op jit(solution)/shard_map/while/body/eval_jaxpr/scatter-add | solution.py:78
  188.6 1.8 convert.18
  190.4 1.3 reshape.297
  191.7 3.4 fusion.39
  195.1 2.8 reshape.360
  197.9 5.4 %scatter_custom_fusion.3 = f32[64,8192]{1,0:T(8,128)} fusion(s32[64]{0:T(128)} %fusion.34, f32[64,8192]{1,0:T(8,128)} %reshape.360, f32[]{:T(128)} %constant.58.clone.1), kind=kCustom, calls=%fused_computation.35 | custom fusion | flops 524288 | bytes 2097664 | tf_op jit(solution)/shard_map/while/body/eval_jaxpr/scatter-add | solution.py:78
  203.4 1.7 convert.19
  205.1 1.3 reshape.299
  206.4 3.2 pad_maximum_fusion.1
  209.7 1.1 copy-done.1
  210.8 1.7 fusion.7
  212.6 2.0 fusion.8
  214.7 6.0 %fusion.51 = f32[256,4608]{0,1:T(8,128)} fusion(bf16[256,512]{1,0:T(8,128)(2,1)S(1)} %constant_dynamic-update-slice_fusion, bf16[4608,512]{1,0:T(8,128)(2,1)} %param.15), kind=kOutput, calls=%fused_computation.93 | convolution fusion | flops 1207959552 | bytes 9699328 | tf_op jit(solution)/shard_map/dot_general | solution.py:133
  220.7 25.4 %reduce-scatter.4.cloned.1.call-done = bf16[256,256]{1,0:T(8,128)(2,1)} async-done(((bf16[4096,256]{1,0:T(8,128)(2,1)}), bf16[256,256]{1,0:T(8,128)(2,1)}) %reduce-scatter.4.cloned.1.call-update) | async-done | bytes 131088 | tf_op jit(solution)/shard_map/reduce_scatter | solution.py:122
  246.2 5.4 %convolution_add_fusion.1 = f32[256,4608]{0,1:T(8,128)} fusion(f32[256,4608]{0,1:T(8,128)} %fusion.51, bf16[256,256]{1,0:T(8,128)(2,1)} %reduce-scatter.4.cloned.1.call-done, bf16[4608,256]{1,0:T(8,128)(2,1)S(1)} %copy-done), kind=kOutput, calls=%fused_computation.11 | convolution fusion | flops 605159424 | bytes 11927552 | tf_op jit(solution)/shard_map/dot_general | solution.py:136
  251.6 69.0 %reduce-scatter.6.cloned.1.call-done = bf16[256,256]{1,0:T(8,128)(2,1)} async-done(((bf16[4096,256]{1,0:T(8,128)(2,1)}), bf16[256,256]{1,0:T(8,128)(2,1)}) %reduce-scatter.6.cloned.1.call-update) | async-done | bytes 131088 | tf_op jit(solution)/shard_map/reduce_scatter | solution.py:125
  320.5 5.3 %fusion.2 = bf16[256,4608]{0,1:T(8,128)(2,1)} fusion(f32[256,4608]{0,1:T(8,128)} %convolution_add_fusion.1, bf16[256,256]{1,0:T(8,128)(2,1)} %reduce-scatter.6.cloned.1.call-done, bf16[4608,256]{1,0:T(8,128)(2,1)} %param.17), kind=kOutput, calls=%fused_computation.12 | convolution fusion | flops 606339072 | bytes 9568256 | tf_op jit(solution)/shard_map/dot_general | solution.py:139
  325.9 56.8 %reduce-scatter.8.cloned.1.call-done = bf16[256,576]{0,1:T(8,128)(2,1)} async-done(((bf16[256,4608]{0,1:T(8,128)(2,1)}), bf16[256,576]{0,1:T(8,128)(2,1)}) %reduce-scatter.8.cloned.1.call-update) | async-done | bytes 294928 | tf_op jit(solution)/shard_map/reduce_scatter | solution.py:142
  (79 shorter events, 12.2 us)
Async XLA Ops:
  7.2 239.0 %copy-start = (bf16[4608,256]{1,0:T(8,128)(2,1)S(1)}, bf16[4608,256]{1,0:T(8,128)(2,1)}, u32[]{:S(2)}) copy-start(bf16[4608,256]{1,0:T(8,128)(2,1)} %param.16) | copy-start | bytes 7077892
  7.2 53.9 %all-gather.5.cloned.1.call-start = ((), (), s32[]{:S(2)}) async-start(), calls=%async_computation.4 | async-start | bytes 2228224 | tf_op jit(solution)/shard_map/all_gather | solution.py:101
  7.9 102.8 %all-gather.3.cloned.1.call-start = ((), (), s32[]{:S(2)}) async-start(), calls=%async_computation.3 | async-start | bytes 2228224 | tf_op jit(solution)/shard_map/all_gather | solution.py:100
  8.7 237.5 %reduce-scatter.4.cloned.1.call-start = ((), (), s32[]{:S(2)}) async-start(), calls=%async_computation.5 | async-start | bytes 2228224 | tf_op jit(solution)/shard_map/reduce_scatter | solution.py:122
  122.4 3.2 copy-start.13
  129.7 2.6 copy-start.6
  129.7 2.6 copy-start.10
  129.7 2.9 copy-start.14
  129.7 2.9 copy-start.16
  132.7 1.5 copy-start.7
  133.1 1.0 copy-start.2
  149.1 2.9 copy-start.12
  151.9 4.1 %copy-start.5 = (bf16[4,16,64,128]{3,2,1,0:T(8,128)(2,1)S(1)}, bf16[4,16,64,128]{3,2,1,0:T(8,128)(2,1)}, u32[]{:S(2)}) copy-start(bf16[4,16,64,128]{3,2,1,0:T(8,128)(2,1)} %get-tuple-element.84) | copy-start | bytes 3145732
  156.0 2.3 copy-start.8
  156.0 2.4 copy-start.15
  156.0 2.4 copy-start.18
  158.9 1.0 copy-start.3
  176.1 0.9 copy-start.11
  176.1 0.9 copy-start.17
  176.2 144.4 %reduce-scatter.6.cloned.1.call-start = ((), (), s32[]{:S(2)}) async-start(), calls=%async_computation.6 | async-start | bytes 2228224 | tf_op jit(solution)/shard_map/reduce_scatter | solution.py:125
  188.6 3.1 copy-start.9
  209.6 1.2 copy-start.1
  209.6 173.1 %reduce-scatter.8.cloned.1.call-start = ((), (), s32[]{:S(2)}) async-start(), calls=%async_computation.7 | async-start | bytes 2654208 | tf_op jit(solution)/shard_map/reduce_scatter | solution.py:142
  214.7 6.0 %copy-start.4 = (bf16[256,512]{1,0:T(8,128)(2,1)}, bf16[256,512]{1,0:T(8,128)(2,1)S(1)}, u32[]{:S(2)}) copy-start(bf16[256,512]{1,0:T(8,128)(2,1)S(1)} %constant_dynamic-update-slice_fusion) | copy-start | bytes 786436
Sparse Core Ops, SparseCore 0:
  10.4 50.6 all-gather.4
  63.5 47.0 all-gather.2
  176.3 69.8 reduce-scatter.3
  250.6 69.9 reduce-scatter.5
  326.0 56.6 reduce-scatter.7
where the time goes:
time: 391 us; the launch traced here: 389 us
  waiting for transfers between devices  240 us (61%)
  other arithmetic  45.6 us (12%)
  matrix products  44.8 us (11%)
  local copies, waits for them, and re-layouts  44.4 us (11%)
  between operations  14 us (4%)
    reduce_scatter x1, waiting for transfers between devices, body(): lax.psum_scatter(accum_v.astype(jnp.bfloat16), 'ctx', scatter_dimension=0...  69 us
    reduce_scatter x1, waiting for transfers between devices, body(): lax.psum_scatter(partial_input.astype(jnp.bfloat16), 'head', scatter_dime...  56.8 us
    all_gather x1, waiting for transfers between devices, body(): lax.all_gather(keys, 'ctx', axis=0, tiled=True)  44.6 us
    all_gather x1, waiting for transfers between devices, body(): lax.all_gather(values, 'ctx', axis=0, tiled=True)  43 us
    reduce_scatter x1, waiting for transfers between devices, body(): lax.psum_scatter(accum_k.astype(jnp.bfloat16), 'ctx', scatter_dimension=0...  25.4 us
    scatter-add x2, other arithmetic, update_step(): running[0].at[flat_blocks].add(grad_k.reshape(-1, BLOCK * head_dim))  11 us
    scatter-add x2, other arithmetic, update_step(): running[1].at[flat_blocks].add(grad_v.reshape(-1, BLOCK * head_dim))  10.9 us
    sub x2, matrix products, block_grads(): weights = jnp.where(allowed, jnp.exp(scores - row_max), 0.0)  8.19 us
  transfers between devices with their start and end apart: 5, of which 5 were waited for; matrix products, arithmetic and copies ran while one was open for 16% of the time, Pallas kernels for 0%

commit v1 on v0

v1 whole, which is shorter than its diff:
```python
import functools
import math

import jax
import jax.numpy as jnp
from jax import lax
from jax.experimental import pallas as pl
from jax.experimental.pallas import tpu as pltpu
from jax.sharding import PartitionSpec as P

HD = 128
BLOCK = 64
TOPK = 16
NX = 4
ROWS = 256
CHUNK = 4
OUT_W = 576
HALF_W = OUT_W // 2
SCALE = 1.0 / math.sqrt(HD)
NT = (((1,), (1,)), ((), ()))
TN = (((0,), (0,)), ((), ()))
F32 = jnp.float32
BF16 = jnp.bfloat16
N_COPIES = 128


def kernel(
    q_ref, go_ref, k_hbm, v_hbm, ch_ref, inv_ref, wq_hbm, wk_hbm, wv_hbm,
    gq_ref, gk_ref, gv_ref, gi_ref,
    kv00, kv01, kv10, kv11, gs_ref, wt_ref, qb_ref, gb_ref,
    t_ref, p_ref, s_ref, r2_ref, rl_ref, rr_ref, ys_ref, yr_ref,
    wq_ref, wk_ref, wv_ref, acc_ref, pt_ref, yb_ref, zs_ref, z2_ref, zl_ref, zr_ref, zys_ref, zyr_ref,
    send_sem, recv_sem, local_sem,
):
    c = lax.axis_index("ctx")
    h = lax.axis_index("head")
    yh, x, k = c // 8, (c // 2) % 4, c % 2
    z, yl = h // 2, h % 2
    kv_bufs = ((kv00, kv01), (kv10, kv11))

    def ctx_at(p, xx, kk):
        return p * 8 + xx * 2 + kk

    xr, xl, xo = (x + 1) % 4, (x + 3) % 4, (x + 2) % 4
    zr, zl, zo = (z + 1) % 4, (z + 3) % 4, (z + 2) % 4
    py = 1 - yh
    to_right = (ctx_at(yh, xr, k), h)
    to_left = (ctx_at(yh, xl, k), h)
    to_y = (ctx_at(py, x, k), h)
    to_core = (ctx_at(yh, x, 1 - k), h)
    to_zr = (c, zr * 2 + yl)
    to_zl = (c, zl * 2 + yl)
    to_yl = (c, z * 2 + (1 - yl))

    started = []

    def send(src, dst, where):
        i = len(started)
        copy = pltpu.make_async_remote_copy(
            src_ref=src,
            dst_ref=dst,
            send_sem=send_sem.at[i],
            recv_sem=recv_sem.at[i],
            device_id=where,
            device_id_type=pl.DeviceIdType.MESH,
        )
        copy.start()
        started.append(copy)
        return copy

    own_copies = []
    n_local = 0
    for g in range(2):
        for kv in range(2):
            src = (k_hbm, v_hbm)[kv]
            group = []
            for b in range(CHUNK):
                copy = pltpu.make_async_copy(
                    src.at[pl.ds(b * BLOCK, BLOCK), pl.ds(g * HD, HD)],
                    kv_bufs[g][kv].at[c * CHUNK + b],
                    local_sem.at[n_local],
                )
                n_local += 1
                copy.start()
                group.append(copy)
            own_copies.append(group)
    weight_copies = []
    for src, dst in ((wq_hbm, wq_ref), (wk_hbm, wk_ref), (wv_hbm, wv_ref)):
        copy = pltpu.make_async_copy(src, dst, local_sem.at[n_local])
        n_local += 1
        copy.start()
        weight_copies.append(copy)

    barrier = pltpu.get_barrier_semaphore()
    partners = (to_right, to_left, to_y, to_core, to_zr, to_zl, to_yl)
    for where in partners:
        pl.semaphore_signal(barrier, inc=1, device_id=where, device_id_type=pl.DeviceIdType.MESH)
    pl.semaphore_wait(barrier, len(partners))

    units = [(g, kv) for g in range(2) for kv in range(2)]

    def slot(u, idx):
        g, kv = units[u]
        return kv_bufs[g][kv].at[pl.ds(pl.multiple_of(idx * CHUNK, CHUNK), CHUNK)]

    def put(u, idx, where):
        return send(slot(u, idx), slot(u, idx), where)

    near, from_y, forwarded, gather_core = {}, {}, {}, []
    for u in range(4):
        for copy in own_copies[u]:
            copy.wait()
        near[u] = (put(u, c, to_right), put(u, c, to_left))
        from_y[u] = put(u, c, to_y)
        gather_core.append(put(u, c, to_core))

    def relay_plane(u, plane, arrivals):
        a_right, a_left = arrivals
        a_right.wait_recv()
        if units[u][1] == 0:
            far = put(u, ctx_at(plane, xl, k), to_right)
        gather_core.append(put(u, ctx_at(plane, xl, k), to_core))
        a_left.wait_recv()
        if units[u][1] == 1:
            far = put(u, ctx_at(plane, xr, k), to_left)
        gather_core.append(put(u, ctx_at(plane, xr, k), to_core))
        return far

    def relay_far(u, plane, far):
        far.wait_recv()
        gather_core.append(put(u, ctx_at(plane, xo, k), to_core))

    far0, near1, far1 = {}, {}, {}
    for u in range(4):
        far0[u] = relay_plane(u, yh, near[u])
        from_y[u].wait_recv()
        yi = ctx_at(py, x, k)
        near1[u] = (put(u, yi, to_right), put(u, yi, to_left))
        gather_core.append(put(u, yi, to_core))
    for u in range(4):
        relay_far(u, yh, far0[u])
    for u in range(4):
        far1[u] = relay_plane(u, py, near1[u])
    for u in range(4):
        relay_far(u, py, far1[u])
    for copy in gather_core:
        copy.wait_recv()

    base = lax.broadcasted_iota(jnp.int32, (BLOCK, HD), 0) - (
        lax.broadcasted_iota(jnp.int32, (BLOCK, HD), 1) % BLOCK
    )

    def attend(g, q):
        own = c * CHUNK + q
        rows = pl.ds(pl.multiple_of(q * BLOCK, BLOCK), BLOCK)
        qb = jnp.concatenate([q_ref[rows, pl.ds((2 * g + i) * HD, HD)] for i in range(2)], axis=0)
        gb = jnp.concatenate([go_ref[rows, pl.ds((2 * g + i) * HD, HD)] for i in range(2)], axis=0)
        qb_ref[g, q] = qb
        gb_ref[g, q] = gb
        blocks = [ch_ref[q * 32 + g * TOPK + s] for s in range(TOPK)]
        kc = jnp.concatenate([kv_bufs[g][0][b] for b in blocks], axis=0)
        scores = SCALE * lax.dot_general(kc, qb, NT, preferred_element_type=F32)
        scores = jnp.concatenate(
            [
                jnp.where(
                    base <= (own - blocks[s]) * BLOCK,
                    scores[s * BLOCK : (s + 1) * BLOCK],
                    -1e30,
                )
                for s in range(TOPK)
            ],
            axis=0,
        )
        top = jnp.max(scores, axis=0, keepdims=True)
        weights = jnp.exp(scores - top)
        weights = weights * (1.0 / jnp.sum(weights, axis=0, keepdims=True))
        low = weights.astype(BF16)
        vc = jnp.concatenate([kv_bufs[g][1][b] for b in blocks], axis=0)
        grad_w = lax.dot_general(vc, gb, NT, preferred_element_type=F32)
        deltas = jnp.sum(low.astype(F32) * grad_w, axis=0, keepdims=True)
        grad_s = (weights * (grad_w - deltas)).astype(BF16)
        grad_q = SCALE * lax.dot_general(grad_s, kc, TN, preferred_element_type=F32)
        for i in range(2):
            gq_ref[rows, pl.ds((2 * g + i) * HD, HD)] = grad_q[i * BLOCK : (i + 1) * BLOCK].astype(BF16)
        for s in range(TOPK):
            gs_ref[g, q, s] = grad_s[s * BLOCK : (s + 1) * BLOCK]
            wt_ref[g, q, s] = low[s * BLOCK : (s + 1) * BLOCK]

    def terms(g):
        for q in range(CHUNK):
            gs_ref[g, q, TOPK] = jnp.zeros((BLOCK, HD), BF16)
            wt_ref[g, q, TOPK] = jnp.zeros((BLOCK, HD), BF16)

        def body(i, carry):
            for kv, (src, rhs) in enumerate(((gs_ref, qb_ref), (wt_ref, gb_ref))):
                right = jnp.concatenate([rhs[g, q] for q in range(CHUNK)], axis=0)
                lines = []
                for b in range(2 * CHUNK):
                    j = i * (2 * CHUNK) + b
                    lines.append(
                        jnp.concatenate(
                            [src[g, q, inv_ref[g * 256 + q * 64 + j]] for q in range(CHUNK)], axis=1
                        )
                    )
                out = jnp.dot(jnp.concatenate(lines, axis=0), right, preferred_element_type=F32)
                if kv == 0:
                    out = SCALE * out
                out = out.astype(BF16)
                t_ref[2 * g + kv, 0, i] = out[:ROWS]
                t_ref[2 * g + kv, 1, i] = out[ROWS:]
            return carry

        lax.fori_loop(0, 8, body, 0)

    core_sums = {}
    for g in range(2):
        def step(q, carry, g=g):
            attend(g, q)
            return carry

        lax.fori_loop(0, CHUNK, step, 0)
        terms(g)
        for kv in range(2):
            u = 2 * g + kv
            core_sums[u] = send(t_ref.at[u, 1 - k], p_ref.at[u], to_core)

    def ring_start(way, mine, r2, rl, rr, places, ends):
        here, right, left, across = places
        go_right, go_left = ends
        if way == 0:
            far = send(mine.at[across], r2, go_right)
            direct = send(mine.at[left], rr, go_left)
        else:
            far = send(mine.at[across], r2, go_left)
            direct = send(mine.at[right], rl, go_right)
        return far, direct

    def ring_relay(way, mine, r2, rl, rr, places, ends, flying):
        here, right, left, across = places
        go_right, go_left = ends
        far, direct = flying
        far.wait_recv()
        i = right if way == 0 else left
        mine[i] = (mine[i].astype(F32) + r2[...].astype(F32)).astype(BF16)
        last = send(mine.at[i], rl if way == 0 else rr, go_right if way == 0 else go_left)
        return last, direct

    def ring_end(mine, rl, rr, places, flying):
        for copy in flying:
            copy.wait_recv()
        return mine[places[0]].astype(F32) + rl[...].astype(F32) + rr[...].astype(F32)

    x_places, x_ends = (x, xr, xl, xo), (to_right, to_left)
    z_places, z_ends = (z, zr, zl, zo), (to_zr, to_zl)

    def x_args(u, plane, n):
        return s_ref.at[u, plane], r2_ref.at[u, n], rl_ref.at[u, n], rr_ref.at[u, n], x_places, x_ends

    flying = {}
    for u in range(4):
        core_sums[u].wait_recv()
        for plane in range(2):
            for xx in range(4):
                i = plane * 4 + xx
                s_ref[u, plane, xx] = (
                    t_ref[u, k, i].astype(F32) + p_ref[u, i].astype(F32)
                ).astype(BF16)
        flying[u, 0] = ring_start(u % 2, *x_args(u, py, 0))
    for u in range(4):
        flying[u, 1] = ring_start(u % 2, *x_args(u, yh, 1))

    for copy in weight_copies:
        copy.wait()

    def query_part(i, carry):
        rows = pl.ds(pl.multiple_of(i * OUT_W, OUT_W), OUT_W)
        acc_ref[rows, :] = lax.dot_general(wq_ref[rows, :], gq_ref[...], NT, preferred_element_type=F32)
        return carry

    lax.fori_loop(0, 8, query_part, 0)

    for u in range(4):
        flying[u, 0] = ring_relay(u % 2, *x_args(u, py, 0), flying[u, 0])
    from_plane = {}
    for u in range(4):
        flying[u, 1] = ring_relay(u % 2, *x_args(u, yh, 1), flying[u, 1])
    for u in range(4):
        mine, _, rl, rr, places, _ = x_args(u, py, 0)
        ys_ref[u] = ring_end(mine, rl, rr, places, flying[u, 0]).astype(BF16)
        from_plane[u] = send(ys_ref.at[u], yr_ref.at[u], to_y)
    for u in range(4):
        g, kv = units[u]
        mine, _, rl, rr, places, _ = x_args(u, yh, 1)
        total = ring_end(mine, rl, rr, places, flying[u, 1])
        from_plane[u].wait_recv()
        total = total + yr_ref[u].astype(F32)
        (gk_ref, gv_ref)[kv][:, pl.ds(g * HD, HD)] = total.astype(BF16)

    def key_value_part(i, carry):
        rows = pl.ds(pl.multiple_of(i * OUT_W, OUT_W), OUT_W)
        out = acc_ref[rows, :]
        out = out + lax.dot_general(wk_ref[rows, :], gk_ref[...], NT, preferred_element_type=F32)
        out = out + lax.dot_general(wv_ref[rows, :], gv_ref[...], NT, preferred_element_type=F32)
        out = out.astype(BF16)
        for t in range(2):
            for w in range(2):
                pt_ref[t, w, i % 2, i // 2] = out[w * HALF_W : (w + 1) * HALF_W, t * HD : (t + 1) * HD]
        return carry

    lax.fori_loop(0, 8, key_value_part, 0)

    def z_args(n, mine):
        return mine, z2_ref.at[n], zl_ref.at[n], zr_ref.at[n], z_places, z_ends

    y_first = [send(pt_ref.at[1, w, 1 - yl], yb_ref.at[w], to_yl) for w in range(2)]
    z_work = {}
    for w in range(2):
        z_work[w] = (w, z_args(w, pt_ref.at[0, w, 1 - yl]))
        z_work[2 + w] = (w, z_args(2 + w, pt_ref.at[0, w, yl]))
        z_work[4 + w] = (w, z_args(4 + w, zs_ref.at[w]))
    fly = {n: ring_start(z_work[n][0], *z_work[n][1]) for n in range(4)}
    for n in range(2):
        fly[n] = ring_relay(z_work[n][0], *z_work[n][1], fly[n])
    for w in range(2):
        y_first[w].wait_recv()
        for i in range(4):
            zs_ref[w, i] = (pt_ref[1, w, yl, i].astype(F32) + yb_ref[w, i].astype(F32)).astype(BF16)
        fly[4 + w] = ring_start(w, *z_work[4 + w][1])
    y_last = []
    for w in range(2):
        mine, _, a, b, places, _ = z_work[w][1]
        zys_ref[w] = ring_end(mine, a, b, places, fly[w]).astype(BF16)
        y_last.append(send(zys_ref.at[w], zyr_ref.at[w], to_yl))
    for n in range(2, 6):
        fly[n] = ring_relay(z_work[n][0], *z_work[n][1], fly[n])
    for w in range(2):
        mine, _, a, b, places, _ = z_work[2 + w][1]
        total = ring_end(mine, a, b, places, fly[2 + w])
        y_last[w].wait_recv()
        total = total + zyr_ref[w].astype(F32)
        gi_ref[pl.ds(w * HALF_W, HALF_W), pl.ds(0, HD)] = total.astype(BF16)
    for w in range(2):
        mine, _, a, b, places, _ = z_work[4 + w][1]
        total = ring_end(mine, a, b, places, fly[4 + w])
        gi_ref[pl.ds(w * HALF_W, HALF_W), pl.ds(HD, HD)] = total.astype(BF16)

    for copy in started:
        copy.wait_send()


def body(queries, keys, values, grad_out, chosen, w_query, w_key, w_value):
    slots = jnp.arange(TOPK, dtype=jnp.int32)[None, None, :, None]
    names = jnp.arange(64, dtype=jnp.int32)[None, None, None, :]
    inverse = jnp.min(jnp.where(chosen[..., None] == names, slots, TOPK), axis=2)
    inverse = inverse.transpose(1, 0, 2).reshape(-1)
    vmem = pl.BlockSpec(memory_space=pltpu.VMEM)
    smem = pl.BlockSpec(memory_space=pltpu.SMEM)
    hbm = pl.BlockSpec(memory_space=pl.ANY)
    shape = jax.ShapeDtypeStruct
    buf = lambda *dims: pltpu.VMEM(dims, BF16)
    chunk = (ROWS, HD)
    zc = (HALF_W, HD)
    grad_queries, grad_keys, grad_values, grad_input = pl.pallas_call(
        kernel,
        out_shape=(
            shape((ROWS, 512), BF16),
            shape((ROWS, 256), BF16),
            shape((ROWS, 256), BF16),
            shape((OUT_W, ROWS), BF16),
        ),
        in_specs=[vmem, vmem, hbm, hbm, smem, smem, hbm, hbm, hbm],
        out_specs=(vmem, vmem, vmem, vmem),
        scratch_shapes=[
            buf(64, BLOCK, HD), buf(64, BLOCK, HD), buf(64, BLOCK, HD), buf(64, BLOCK, HD),
            buf(2, CHUNK, TOPK + 1, BLOCK, HD), buf(2, CHUNK, TOPK + 1, BLOCK, HD),
            buf(2, CHUNK, HD, HD), buf(2, CHUNK, HD, HD),
            buf(4, 2, 8, *chunk), buf(4, 8, *chunk), buf(4, 2, 4, *chunk),
            buf(4, 2, *chunk), buf(4, 2, *chunk), buf(4, 2, *chunk), buf(4, *chunk), buf(4, *chunk),
            buf(4608, 512), buf(4608, 256), buf(4608, 256), pltpu.VMEM((4608, ROWS), F32),
            buf(2, 2, 2, 4, *zc), buf(2, 4, *zc), buf(2, 4, *zc),
            buf(6, *zc), buf(6, *zc), buf(6, *zc), buf(2, *zc), buf(2, *zc),
            pltpu.SemaphoreType.DMA((N_COPIES,)),
            pltpu.SemaphoreType.DMA((N_COPIES,)),
            pltpu.SemaphoreType.DMA((19,)),
        ],
        compiler_params=pltpu.CompilerParams(
            collective_id=0, has_side_effects=True, vmem_limit_bytes=60 * 1024 * 1024
        ),
    )(queries, grad_out, keys, values, chosen.reshape(-1), inverse, w_query, w_key, w_value)
    return grad_queries, grad_keys, grad_values, grad_input.T


def solution(mesh):
    both = P("ctx", "head")
    return jax.shard_map(
        body,
        mesh=mesh,
        in_specs=(both, both, both, both, P("ctx", "head", None)) + (P(None, "head"),) * 3,
        out_specs=(both, both, both, both),
        check_vma=False,
    )
```

time: 391 us -> 105 us (0.27)
  waiting for transfers between devices: 240 us -> 0 us
  Pallas kernels: 0 us -> 93.8 us
  other arithmetic: 45.6 us -> 0.79 us
  matrix products: 44.8 us -> 0 us
  local copies, waits for them, and re-layouts: 44.4 us -> 8.44 us
  between operations: 14 us -> 0.65 us
    reduce_scatter x3 -> x0, waiting for transfers between devices: 151 us -> none  [the longest x1 69 us: body(): lax.psum_scatter(accum_v.astype(jnp.bfloat16), 'ctx', scatter_dimension=0...]
    pallas_call x0 -> x1, Pallas kernels: none -> 93.8 us  [body(): pl.pallas_call(kernel, out_shape=(shape((ROWS, 512), BF16), shape((ROWS,...]
    all_gather x2 -> x0, waiting for transfers between devices: 87.6 us -> none  [the longest x1 44.6 us: body(): lax.all_gather(keys, 'ctx', axis=0, tiled=True)]
    dot_general x13 -> x0, matrix products: 36.6 us -> none  [the longest x2 6.74 us: block_grads(): lax.dot_general(weights_low, grad_rows, across, preferred_element_type=jn...]
    scatter-add x4 -> x0, other arithmetic: 21.9 us -> none  [the longest x2 11 us: update_step(): running[0].at[flat_blocks].add(grad_k.reshape(-1, BLOCK * head_dim))]
    reshape x16 -> x2, local copies, waits for them, and re-layouts: 19.8 us -> 1.94 us  [the longest x1 1.28 us: body(): chosen.reshape(-1)]
    gather x4 -> x0, local copies, waits for them, and re-layouts: 10.6 us -> none  [the longest x2 5.77 us: block_grads(): chosen_keys = jnp.take(key_blocks, picked, axis=0).reshape(-1, head_dim)]
    slice x5 -> x0, local copies, waits for them, and re-layouts: 8.86 us -> none  [the longest x1 3.09 us: body(): key_all[:, key_cols]]
  transfers between devices with their start and end apart: 5 -> 0, of which waited for: 5 -> 0; matrix products, arithmetic and copies ran while one was open for 16% -> 0% of each run, Pallas kernels for 0% -> 0%
where the time goes in v1:
time: 105 us; the launch traced here: 104 us
  Pallas kernels  93.8 us (89%)
  local copies, waits for them, and re-layouts  8.44 us (8%)
    pallas_call x1, Pallas kernels, body(): pl.pallas_call(kernel, out_shape=(shape((ROWS, 512), BF16), shape((ROWS,...  93.8 us
    unnamed x4, local copies, waits for them, and re-layouts  6.5 us

profile of v1, /device:TPU:0, one launch (start us, length us, event | category | flops | bytes accessed | tf_op | source)
XLA Modules:
  0.0 103.6 jit_solution(5271546415506966934)
XLA Ops:
  0.6 1.3 %reshape.15.ch_ref = s32[128]{0:T(128)} reshape(s32[4,2,16]{2,1,0:T(2,128)} %param.12) | data formatting | bytes 1024 | tf_op jit(solution)/shard_map/reshape | solution.py:389
  1.9 0.8 select_reduce_fusion
  2.7 0.7 reshape.16.inv_ref
  3.4 93.8 %shard_map.111 = (bf16[256,512]{1,0:T(8,128)(2,1)}, bf16[256,256]{1,0:T(8,128)(2,1)}, bf16[256,256]{1,0:T(8,128)(2,1)}, bf16[576,256]{1,0:T(8,128)(2,1)}) custom-call(bf16[256,512]{1,0:T(8,128)(2,1)} %q_ref.1, bf16[256,512]{1,0:T(8,128)(2,1)} %go_ref.1, bf16[256,256]{1,0:T(8,128)(2,1)} %k_hbm.1, bf16[256,256]{1,0:T(8,128)(2,1)} %v_hbm.1, ...), custom_call_target="tpu_custom_call" | custom-call | tf_op jit(solution)/shard_map/pallas_call | solution.py:363
  97.1 1.7 %copy.17 = bf16[256,512]{1,0:T(8,128)(2,1)} copy(bf16[256,512]{1,0:T(8,128)(2,1)} %get-tuple-element.16) | data formatting | bytes 524288
  98.8 1.6 %copy.18 = bf16[256,256]{1,0:T(8,128)(2,1)} copy(bf16[256,256]{1,0:T(8,128)(2,1)} %get-tuple-element.17) | data formatting | bytes 262144
  100.4 1.6 %copy.19 = bf16[256,256]{1,0:T(8,128)(2,1)} copy(bf16[256,256]{1,0:T(8,128)(2,1)} %get-tuple-element.18) | data formatting | bytes 262144
  101.9 1.7 %copy.20 = bf16[256,576]{0,1:T(8,128)(2,1)} copy(bf16[256,576]{0,1:T(8,128)(2,1)} %bitcast.2) | data formatting | bytes 589824
  (1 shorter events, 0.0 us)

commit v2 on v1

v2 whole, which is shorter than its diff:
```python
import functools
import math

import jax
import jax.numpy as jnp
from jax import lax
from jax.experimental import pallas as pl
from jax.experimental.pallas import tpu as pltpu
from jax.sharding import PartitionSpec as P

HD = 128
BLOCK = 64
TOPK = 16
NX = 4
ROWS = 256
CHUNK = 4
OUT_W = 576
HALF_W = OUT_W // 2
SCALE = 1.0 / math.sqrt(HD)
NT = (((1,), (1,)), ((), ()))
TN = (((0,), (0,)), ((), ()))
F32 = jnp.float32
BF16 = jnp.bfloat16
N_COPIES = 144


def kernel(
    q_hbm, go_hbm, k_hbm, v_hbm, ch_ref, inv_ref, wq_hbm, wk_hbm, wv_hbm,
    gq_hbm, gk_hbm, gv_hbm, gi_hbm,
    kv00, kv01, kv10, kv11, q_ref, go_ref, gq_ref, gk_ref, gv_ref, gi_ref,
    gs_ref, wt_ref, qb_ref, gb_ref,
    t_ref, p_ref, s_ref, xa_ref, xf_ref, xl_ref, xr_ref, xs_ref, xy_ref,
    wq_ref, wk_ref, wv_ref, acc_ref, pt_ref, za_ref, zf_ref, zl_ref, zr_ref, zs_ref, zy_ref,
    send_sem, recv_sem, local_sem,
):
    c = lax.axis_index("ctx")
    h = lax.axis_index("head")
    yh, x, k = c // 8, (c // 2) % 4, c % 2
    z, yl = h // 2, h % 2
    kv_bufs = ((kv00, kv01), (kv10, kv11))

    def ctx_at(p, xx, kk):
        return p * 8 + xx * 2 + kk

    xr, xl, xo = (x + 1) % 4, (x + 3) % 4, (x + 2) % 4
    zr, zl, zo = (z + 1) % 4, (z + 3) % 4, (z + 2) % 4
    py = 1 - yh
    to_right = (ctx_at(yh, xr, k), h)
    to_left = (ctx_at(yh, xl, k), h)
    to_y = (ctx_at(py, x, k), h)
    to_core = (ctx_at(yh, x, 1 - k), h)
    to_zr = (c, zr * 2 + yl)
    to_zl = (c, zl * 2 + yl)
    to_yl = (c, z * 2 + (1 - yl))

    started = []

    def plan(src, dst, where):
        i = len(started)
        copy = pltpu.make_async_remote_copy(
            src_ref=src,
            dst_ref=dst,
            send_sem=send_sem.at[i],
            recv_sem=recv_sem.at[i],
            device_id=where,
            device_id_type=pl.DeviceIdType.MESH,
        )
        started.append(copy)
        return copy

    def send(src, dst, where):
        copy = plan(src, dst, where)
        copy.start()
        return copy

    barrier = pltpu.get_barrier_semaphore()
    partners = (to_right, to_left, to_y, to_core, to_zr, to_zl, to_yl)
    for where in partners:
        pl.semaphore_signal(barrier, inc=1, device_id=where, device_id_type=pl.DeviceIdType.MESH)

    own_copies = []
    n_local = 0
    for g in range(2):
        for kv in range(2):
            src = (k_hbm, v_hbm)[kv]
            group = []
            for b in range(CHUNK):
                copy = pltpu.make_async_copy(
                    src.at[pl.ds(b * BLOCK, BLOCK), pl.ds(g * HD, HD)],
                    kv_bufs[g][kv].at[c * CHUNK + b],
                    local_sem.at[n_local],
                )
                n_local += 1
                copy.start()
                group.append(copy)
            own_copies.append(group)

    def local(src, dst):
        nonlocal n_local
        copy = pltpu.make_async_copy(src, dst, local_sem.at[n_local])
        n_local += 1
        copy.start()
        return copy

    query_copies = [local(q_hbm, q_ref), local(go_hbm, go_ref)]
    weight_copies = [local(wq_hbm, wq_ref), local(wk_hbm, wk_ref), local(wv_hbm, wv_ref)]
    out_copies = []

    pl.semaphore_wait(barrier, len(partners))

    units = [(g, kv) for g in range(2) for kv in range(2)]

    def slot(u, idx):
        g, kv = units[u]
        return kv_bufs[g][kv].at[pl.ds(pl.multiple_of(idx * CHUNK, CHUNK), CHUNK)]

    def put(u, idx, where):
        return plan(slot(u, idx), slot(u, idx), where)

    g_near, g_far, g_core, g_y = {}, {}, {}, {}
    for u in range(4):
        g_y[u] = put(u, c, to_y)
        for n, plane in enumerate((yh, py)):
            first = ctx_at(plane, x, k)
            g_near[u, n] = (put(u, first, to_right), put(u, first, to_left))
            if n == 1:
                g_far[u, n] = put(u, ctx_at(yh, xo, k), to_y)
            elif units[u][1] == 0:
                g_far[u, n] = put(u, ctx_at(plane, xl, k), to_right)
            else:
                g_far[u, n] = put(u, ctx_at(plane, xr, k), to_left)
            g_core[u, n] = [put(u, ctx_at(plane, xx, k), to_core) for xx in (x, xl, xr, xo)]

    def gather_first(u):
        for copy in own_copies[u]:
            copy.wait()
        g_near[u, 0][0].start()
        g_near[u, 0][1].start()
        g_y[u].start()
        g_core[u, 0][0].start()

    def gather_relay(u, n):
        for side in range(2):
            g_near[u, n][side].wait_recv()
            if n == 0 and units[u][1] == side:
                g_far[u, 0].start()
            g_core[u, n][1 + side].start()

    def gather_y(u):
        g_y[u].wait_recv()
        g_near[u, 1][0].start()
        g_near[u, 1][1].start()
        g_core[u, 1][0].start()

    def gather_far(u, n):
        g_far[u, n].wait_recv()
        if n == 0:
            g_far[u, 1].start()
        g_core[u, n][3].start()

    def gather_end(u):
        for n in range(2):
            for copy in g_core[u, n]:
                copy.wait_recv()

    def each(step, *names):
        for name in names:
            step(*name)

    each(gather_first, (0,), (1,))
    for u in (0, 1):
        gather_relay(u, 0)
        gather_y(u)
    each(gather_first, (2,), (3,))
    each(gather_far, (0, 0), (1, 0))
    each(gather_relay, (0, 1), (1, 1))
    for u in (2, 3):
        gather_relay(u, 0)
        gather_y(u)
    each(gather_far, (0, 1), (1, 1))
    each(gather_end, (0,), (1,))
    for copy in query_copies:
        copy.wait()

    base = lax.broadcasted_iota(jnp.int32, (BLOCK, HD), 0) - (
        lax.broadcasted_iota(jnp.int32, (BLOCK, HD), 1) % BLOCK
    )

    def attend(g, q):
        own = c * CHUNK + q
        rows = pl.ds(pl.multiple_of(q * BLOCK, BLOCK), BLOCK)
        qb = jnp.concatenate([q_ref[rows, pl.ds((2 * g + i) * HD, HD)] for i in range(2)], axis=0)
        gb = jnp.concatenate([go_ref[rows, pl.ds((2 * g + i) * HD, HD)] for i in range(2)], axis=0)
        qb_ref[g, q] = qb
        gb_ref[g, q] = gb
        blocks = [ch_ref[q, g, s] for s in range(TOPK)]
        kc = jnp.concatenate([kv_bufs[g][0][b] for b in blocks], axis=0)
        scores = SCALE * lax.dot_general(kc, qb, NT, preferred_element_type=F32)
        scores = jnp.concatenate(
            [
                jnp.where(
                    base <= (own - blocks[s]) * BLOCK,
                    scores[s * BLOCK : (s + 1) * BLOCK],
                    -1e30,
                )
                for s in range(TOPK)
            ],
            axis=0,
        )
        top = jnp.max(scores, axis=0, keepdims=True)
        weights = jnp.exp(scores - top)
        weights = weights * (1.0 / jnp.sum(weights, axis=0, keepdims=True))
        low = weights.astype(BF16)
        vc = jnp.concatenate([kv_bufs[g][1][b] for b in blocks], axis=0)
        grad_w = lax.dot_general(vc, gb, NT, preferred_element_type=F32)
        deltas = jnp.sum(low.astype(F32) * grad_w, axis=0, keepdims=True)
        grad_s = (weights * (grad_w - deltas)).astype(BF16)
        grad_q = SCALE * lax.dot_general(grad_s, kc, TN, preferred_element_type=F32)
        for i in range(2):
            gq_ref[rows, pl.ds((2 * g + i) * HD, HD)] = grad_q[i * BLOCK : (i + 1) * BLOCK].astype(BF16)
        for s in range(TOPK):
            gs_ref[g, q, s] = grad_s[s * BLOCK : (s + 1) * BLOCK]
            wt_ref[g, q, s] = low[s * BLOCK : (s + 1) * BLOCK]

    for g in range(2):
        for q in range(CHUNK):
            gs_ref[g, q, TOPK] = jnp.zeros((BLOCK, HD), BF16)
            wt_ref[g, q, TOPK] = jnp.zeros((BLOCK, HD), BF16)

    def terms(g, plane):
        def body(i, carry):
            for kv, (src, rhs) in enumerate(((gs_ref, qb_ref), (wt_ref, gb_ref))):
                right = jnp.concatenate([rhs[g, q] for q in range(CHUNK)], axis=0)
                lines = []
                for b in range(2 * CHUNK):
                    j = (plane * 4 + i) * (2 * CHUNK) + b
                    lines.append(
                        jnp.concatenate(
                            [src[g, q, inv_ref[q, g, j]] for q in range(CHUNK)], axis=1
                        )
                    )
                out = jnp.dot(jnp.concatenate(lines, axis=0), right, preferred_element_type=F32)
                if kv == 0:
                    out = SCALE * out
                out = out.astype(BF16)
                t_ref[2 * g + kv, plane, 0, i] = out[:ROWS]
                t_ref[2 * g + kv, plane, 1, i] = out[ROWS:]
            return carry

        lax.fori_loop(0, 4, body, 0)

    planes = (py, yh)
    core_sums = {
        (u, n): plan(t_ref.at[u, planes[n], 1 - k], p_ref.at[u, planes[n]], to_core)
        for u in range(4)
        for n in range(2)
    }

    class Sum:
        def __init__(self, way, theirs, mine, bufs, places, ends, over):
            self.way, self.theirs, self.mine, self.bufs = way, theirs, mine, bufs
            self.here, right, left, across = places
            self.across = across
            go_right, go_left = ends
            first, far, l0, r0, l1, r1, stage, last = bufs
            self.first = plan(theirs.at[across], first, over)
            self.theirs_right = plan(theirs.at[right], l1, go_right)
            self.theirs_left = plan(theirs.at[left], r1, go_left)
            self.far = plan(mine.at[across], far, go_right if way == 0 else go_left)
            self.mine_right = plan(mine.at[right], l0, go_right)
            self.mine_left = plan(mine.at[left], r0, go_left)
            self.relayed, self.direct = (
                (self.mine_right, self.mine_left) if way == 0 else (self.mine_left, self.mine_right)
            )
            self.relay_at = right if way == 0 else left
            self.over = plan(stage, last, over)

        def start_theirs(self):
            self.first.start()
            self.theirs_right.start()
            self.theirs_left.start()

        def start_mine(self):
            self.direct.start()

        def add(self, i, buf):
            self.mine[i] = (self.mine[i].astype(F32) + buf[...].astype(F32)).astype(BF16)

        def go_far(self):
            self.first.wait_recv()
            self.add(self.across, self.bufs[0])
            self.far.start()

        def cross(self):
            _, _, _, _, l1, r1, stage, _ = self.bufs
            self.theirs_right.wait_recv()
            self.theirs_left.wait_recv()
            total = self.theirs[self.here].astype(F32) + l1[...].astype(F32) + r1[...].astype(F32)
            stage[...] = total.astype(BF16)
            self.over.start()

        def relay(self):
            self.far.wait_recv()
            self.add(self.relay_at, self.bufs[1])
            self.relayed.start()

        def end(self):
            _, _, l0, r0, _, _, _, last = self.bufs
            self.mine_right.wait_recv()
            self.mine_left.wait_recv()
            total = self.mine[self.here].astype(F32) + l0[...].astype(F32) + r0[...].astype(F32)
            self.over.wait_recv()
            return total + last[...].astype(F32)

    x_sums = [
        Sum(
            u % 2, s_ref.at[u, py], s_ref.at[u, yh],
            (xa_ref.at[u], xf_ref.at[u], xl_ref.at[u, 0], xr_ref.at[u, 0],
             xl_ref.at[u, 1], xr_ref.at[u, 1], xs_ref.at[u], xy_ref.at[u]),
            (x, xr, xl, xo), (to_right, to_left), to_y,
        )
        for u in range(4)
    ]

    def core_sum(u, n):
        plane = planes[n]
        core_sums[u, n].wait_recv()
        for xx in range(4):
            s_ref[u, plane, xx] = (
                t_ref[u, plane, k, xx].astype(F32) + p_ref[u, plane, xx].astype(F32)
            ).astype(BF16)
        if n == 0:
            x_sums[u].start_theirs()
        else:
            x_sums[u].start_mine()

    def sum_end(u):
        g, kv = units[u]
        (gk_ref, gv_ref)[kv][:, pl.ds(g * HD, HD)] = x_sums[u].end().astype(BF16)

    def do(names, *steps):
        for step in steps:
            for u in names:
                getattr(x_sums[u], step)()

    def core_start(g, n):
        core_sums[2 * g, n].start()
        core_sums[2 * g + 1, n].start()

    hooks = {
        (0, 1): lambda: (each(gather_far, (2, 0), (3, 0)), each(gather_relay, (2, 1), (3, 1))),
        (0, 3): lambda: each(gather_far, (2, 1), (3, 1)),
        (1, 1): lambda: each(core_sum, (0, 0), (1, 0), (0, 1), (1, 1)),
        (1, 3): lambda: do((0, 1), "go_far", "cross"),
    }
    for g in range(2):
        if g == 1:
            each(gather_end, (2,), (3,))

        def step(q, carry, g=g):
            for (gg, at), action in hooks.items():
                if gg == g:
                    pl.when(q == at)(lambda action=action: (action(), None)[1])
            attend(g, q)
            return carry

        lax.fori_loop(0, CHUNK, step, 0)
        if g == 1:
            out_copies.append(local(gq_ref, gq_hbm))
        for n in range(2):
            terms(g, planes[n])
            core_start(g, n)
            if g == 1 and n == 0:
                do((0, 1), "relay")
    each(core_sum, (2, 0), (3, 0))

    for copy in weight_copies:
        copy.wait()

    def query_part(i, carry):
        rows = pl.ds(pl.multiple_of(i * OUT_W, OUT_W), OUT_W)
        acc_ref[rows, :] = lax.dot_general(wq_ref[rows, :], gq_ref[...], NT, preferred_element_type=F32)
        return carry

    lax.fori_loop(0, 3, query_part, 0)
    each(core_sum, (2, 1), (3, 1))
    lax.fori_loop(3, 6, query_part, 0)
    do((2, 3), "go_far")
    do((2, 3), "cross")
    lax.fori_loop(6, 8, query_part, 0)
    do((2, 3), "relay")
    each(sum_end, (0,), (1,), (2,), (3,))
    out_copies.append(local(gk_ref, gk_hbm))
    out_copies.append(local(gv_ref, gv_hbm))

    z_places = (z, zr, zl, zo)
    z_sums = [
        Sum(
            w, pt_ref.at[w, 1 - yl], pt_ref.at[w, yl],
            (za_ref.at[w], zf_ref.at[w], zl_ref.at[w, 0], zr_ref.at[w, 0],
             zl_ref.at[w, 1], zr_ref.at[w, 1], zs_ref.at[w], zy_ref.at[w]),
            z_places, (to_zr, to_zl), to_yl,
        )
        for w in range(2)
    ]

    def term_chunk(side, zz):
        i = zz * 2 + side
        rows = pl.ds(pl.multiple_of(i * OUT_W, OUT_W), OUT_W)
        out = acc_ref[rows, :]
        out = out + lax.dot_general(wk_ref[rows, :], gk_ref[...], NT, preferred_element_type=F32)
        out = out + lax.dot_general(wv_ref[rows, :], gv_ref[...], NT, preferred_element_type=F32)
        out = out.astype(BF16)
        for w in range(2):
            pt_ref[w, side, zz] = out[w * HALF_W : (w + 1) * HALF_W]

    def both(step):
        for w in range(2):
            step(z_sums[w])

    term_chunk(1 - yl, zo)
    both(lambda t: t.first.start())
    term_chunk(1 - yl, zr)
    both(lambda t: t.theirs_right.start())
    term_chunk(1 - yl, zl)
    both(lambda t: t.theirs_left.start())
    term_chunk(yl, zl)
    z_sums[0].direct.start()
    term_chunk(yl, zr)
    z_sums[1].direct.start()
    term_chunk(yl, zo)
    both(lambda t: t.go_far())
    term_chunk(1 - yl, z)
    term_chunk(yl, z)
    both(lambda t: t.cross())
    both(lambda t: t.relay())
    for w in range(2):
        gi_ref[pl.ds(w * HALF_W, HALF_W), :] = z_sums[w].end().astype(BF16)
        out_copies.append(
            local(gi_ref.at[pl.ds(w * HALF_W, HALF_W)], gi_hbm.at[pl.ds(w * HALF_W, HALF_W)])
        )

    for copy in out_copies:
        copy.wait()
    for copy in started:
        copy.wait_send()


def write_out(*refs):
    for src, dst in zip(refs[:4], refs[4:]):
        dst[...] = src[...]


def body(queries, keys, values, grad_out, chosen, w_query, w_key, w_value):
    slots = jnp.arange(TOPK, dtype=jnp.int32)[None, None, :, None]
    names = jnp.arange(64, dtype=jnp.int32)[None, None, None, :]
    inverse = jnp.min(jnp.where(chosen[..., None] == names, slots, TOPK), axis=2)
    vmem = pl.BlockSpec(memory_space=pltpu.VMEM)
    smem = pl.BlockSpec(memory_space=pltpu.SMEM)
    hbm = pl.BlockSpec(memory_space=pl.ANY)
    shape = jax.ShapeDtypeStruct
    buf = lambda *dims: pltpu.VMEM(dims, BF16)
    chunk = (ROWS, HD)
    zc = (HALF_W, ROWS)
    outs = pl.pallas_call(
        kernel,
        out_shape=(
            shape((ROWS, 512), BF16),
            shape((ROWS, 256), BF16),
            shape((ROWS, 256), BF16),
            shape((OUT_W, ROWS), BF16),
        ),
        in_specs=[hbm, hbm, hbm, hbm, smem, smem, hbm, hbm, hbm],
        out_specs=(hbm,) * 4,
        scratch_shapes=[
            buf(64, BLOCK, HD), buf(64, BLOCK, HD), buf(64, BLOCK, HD), buf(64, BLOCK, HD),
            buf(ROWS, 512), buf(ROWS, 512), buf(ROWS, 512), buf(ROWS, 256), buf(ROWS, 256), buf(OUT_W, ROWS),
            buf(2, CHUNK, TOPK + 1, BLOCK, HD), buf(2, CHUNK, TOPK + 1, BLOCK, HD),
            buf(2, CHUNK, HD, HD), buf(2, CHUNK, HD, HD),
            buf(4, 2, 2, 4, *chunk), buf(4, 2, 4, *chunk), buf(4, 2, 4, *chunk),
            buf(4, *chunk), buf(4, *chunk), buf(4, 2, *chunk), buf(4, 2, *chunk), buf(4, *chunk), buf(4, *chunk),
            buf(4608, 512), buf(4608, 256), buf(4608, 256), pltpu.VMEM((4608, ROWS), F32),
            buf(2, 2, 4, *zc), buf(2, *zc), buf(2, *zc),
            buf(2, 2, *zc), buf(2, 2, *zc), buf(2, *zc), buf(2, *zc),
            pltpu.SemaphoreType.DMA((N_COPIES,)),
            pltpu.SemaphoreType.DMA((N_COPIES,)),
            pltpu.SemaphoreType.DMA((32,)),
        ],
        compiler_params=pltpu.CompilerParams(
            collective_id=0, has_side_effects=True, vmem_limit_bytes=60 * 1024 * 1024
        ),
    )(queries, grad_out, keys, values, chosen, inverse, w_query, w_key, w_value)
    grad_queries, grad_keys, grad_values, grad_input = pl.pallas_call(
        write_out,
        out_shape=tuple(shape(o.shape, o.dtype) for o in outs),
        in_specs=[vmem] * 4,
        out_specs=(vmem,) * 4,
    )(*outs)
    return grad_queries, grad_keys, grad_values, grad_input.T


def solution(mesh):
    both = P("ctx", "head")
    return jax.shard_map(
        body,
        mesh=mesh,
        in_specs=(both, both, both, both, P("ctx", "head", None)) + (P(None, "head"),) * 3,
        out_specs=(both, both, both, both),
        check_vma=False,
    )
```

time: 105 us -> 83.3 us (0.79)
  Pallas kernels: 93.8 us -> 80.8 us
  local copies, waits for them, and re-layouts: 8.44 us -> 0 us
    pallas_call x1, Pallas kernels: 93.8 us -> 78.7 us  [body(): pl.pallas_call(kernel, out_shape=(shape((ROWS, 512), BF16), shape((ROWS,...]
    unnamed x4 -> x0, local copies, waits for them, and re-layouts: 6.5 us -> none
    pallas_call x0 -> x1, Pallas kernels: none -> 2.07 us  [body(): pl.pallas_call(write_out, out_shape=tuple((shape(o.shape, o.dtype) for o...]
    reshape x2 -> x0, local copies, waits for them, and re-layouts: 1.94 us -> none  [the longest x1 1.28 us: body(): chosen.reshape(-1)]
where the time goes in v2:
time: 83.3 us; the launch traced here: 82.8 us
  Pallas kernels  80.8 us (97%)
  other arithmetic  1.38 us (2%)
    pallas_call x1, Pallas kernels, body(): pl.pallas_call(kernel, out_shape=(shape((ROWS, 512), BF16), shape((ROWS,...  78.7 us
    pallas_call x1, Pallas kernels, body(): pl.pallas_call(write_out, out_shape=tuple((shape(o.shape, o.dtype) for o...  2.07 us

profile of v2, /device:TPU:0, one launch (start us, length us, event | category | flops | bytes accessed | tf_op | source)
XLA Modules:
  0.0 82.8 jit_solution(5635998759747210511)
XLA Ops:
  0.6 1.4 %select_reduce_fusion.inv_ref = s32[4,2,64]{2,1,0:T(2,128)} fusion(s32[4,2,16]{2,1,0:T(2,128)} %ch_ref.1), kind=kLoop, calls=%fused_computation | loop fusion | flops 24064 | bytes 2560 | tf_op jit(solution)/shard_map/reduce_min | solution.py:457
  2.0 78.7 %shard_map.111 = (bf16[256,512]{1,0:T(8,128)(2,1)}, bf16[256,256]{1,0:T(8,128)(2,1)}, bf16[256,256]{1,0:T(8,128)(2,1)}, bf16[576,256]{1,0:T(8,128)(2,1)}) custom-call(bf16[256,512]{1,0:T(8,128)(2,1)} %q_hbm.1, bf16[256,512]{1,0:T(8,128)(2,1)} %go_hbm.1, bf16[256,256]{1,0:T(8,128)(2,1)} %k_hbm.1, bf16[256,256]{1,0:T(8,128)(2,1)} %v_hbm.1, ...), custom_call_target="tpu_custom_call" | custom-call | tf_op jit(solution)/shard_map/pallas_call | solution.py:465
  80.7 2.1 %shard_map.112 = (bf16[256,512]{1,0:T(8,128)(2,1)}, bf16[256,256]{1,0:T(8,128)(2,1)}, bf16[256,256]{1,0:T(8,128)(2,1)}, bf16[576,256]{1,0:T(8,128)(2,1)}) custom-call(bf16[256,512]{1,0:T(8,128)(2,1)} %get-tuple-element.12.refs_0_, bf16[256,256]{1,0:T(8,128)(2,1)} %get-tuple-element.13.refs_1_, bf16[256,256]{1,0:T(8,128)(2,1)} %get-tuple-element.14.refs_2_, ...), custom_call_target="tpu_custom_call" | custom-call | tf_op jit(solution)/shard_map/pallas_call | solution.py:493

commit v3 on v2

--- a/solution.py
+++ b/solution.py
@@ -16,7 +16,9 @@
 CHUNK = 4
 OUT_W = 576
 HALF_W = OUT_W // 2
+HALF_K = TOPK * BLOCK // 2
 SCALE = 1.0 / math.sqrt(HD)
+EXP2_SCALE = SCALE / math.log(2.0)
 NT = (((1,), (1,)), ((), ()))
 TN = (((0,), (0,)), ((), ()))
 F32 = jnp.float32
@@ -25,10 +27,10 @@
 
 
 def kernel(
-    q_hbm, go_hbm, k_hbm, v_hbm, ch_ref, inv_ref, wq_hbm, wk_hbm, wv_hbm,
+    q_hbm, go_hbm, k_hbm, v_hbm, ch_ref, chv_ref, wq_hbm, wk_hbm, wv_hbm,
     gq_hbm, gk_hbm, gv_hbm, gi_hbm,
     kv00, kv01, kv10, kv11, q_ref, go_ref, gq_ref, gk_ref, gv_ref, gi_ref,
-    gs_ref, wt_ref, qb_ref, gb_ref,
+    tm_ref, names_ref, inv_ref,
     t_ref, p_ref, s_ref, xa_ref, xf_ref, xl_ref, xr_ref, xs_ref, xy_ref,
     wq_ref, wk_ref, wv_ref, acc_ref, pt_ref, za_ref, zf_ref, zl_ref, zr_ref, zs_ref, zy_ref,
     send_sem, recv_sem, local_sem,
@@ -106,7 +108,17 @@
     weight_copies = [local(wq_hbm, wq_ref), local(wk_hbm, wk_ref), local(wv_hbm, wv_ref)]
     out_copies = []
 
+    lanes = lax.broadcasted_iota(jnp.int32, (2, HD), 1)
+    for q in range(CHUNK):
+        picked = chv_ref[q]
+        found = jnp.full((2, HD), TOPK, jnp.int32)
+        for n in range(TOPK):
+            found = jnp.where(picked[:, n : n + 1] == lanes, n, found)
+        names_ref[q] = found
+        tm_ref[q, TOPK] = jnp.zeros((BLOCK, 2 * HD), BF16)
+
     pl.semaphore_wait(barrier, len(partners))
+    names_copy = local(names_ref, inv_ref)
 
     units = [(g, kv) for g in range(2) for kv in range(2)]
 
@@ -136,8 +148,10 @@
             copy.wait()
         g_near[u, 0][0].start()
         g_near[u, 0][1].start()
+        g_core[u, 0][0].start()
+
+    def gather_over(u):
         g_y[u].start()
-        g_core[u, 0][0].start()
 
     def gather_relay(u, n):
         for side in range(2):
@@ -167,20 +181,18 @@
         for name in names:
             step(*name)
 
-    each(gather_first, (0,), (1,))
-    for u in (0, 1):
-        gather_relay(u, 0)
-        gather_y(u)
-    each(gather_first, (2,), (3,))
-    each(gather_far, (0, 0), (1, 0))
+    for u in range(4):
+        gather_first(u)
+        gather_over(u)
+    each(gather_relay, *((u, 0) for u in range(4)))
+    each(gather_y, *((u,) for u in range(4)))
+    each(gather_far, *((u, 0) for u in range(4)))
     each(gather_relay, (0, 1), (1, 1))
-    for u in (2, 3):
-        gather_relay(u, 0)
-        gather_y(u)
     each(gather_far, (0, 1), (1, 1))
     each(gather_end, (0,), (1,))
     for copy in query_copies:
         copy.wait()
+    names_copy.wait()
 
     base = lax.broadcasted_iota(jnp.int32, (BLOCK, HD), 0) - (
         lax.broadcasted_iota(jnp.int32, (BLOCK, HD), 1) % BLOCK
@@ -191,16 +203,27 @@
         rows = pl.ds(pl.multiple_of(q * BLOCK, BLOCK), BLOCK)
         qb = jnp.concatenate([q_ref[rows, pl.ds((2 * g + i) * HD, HD)] for i in range(2)], axis=0)
         gb = jnp.concatenate([go_ref[rows, pl.ds((2 * g + i) * HD, HD)] for i in range(2)], axis=0)
-        qb_ref[g, q] = qb
-        gb_ref[g, q] = gb
+        none = jnp.zeros((HD, HD), BF16)
+        pair = jnp.concatenate(
+            [jnp.concatenate([qb, none], axis=1), jnp.concatenate([none, gb], axis=1)], axis=0
+        )
         blocks = [ch_ref[q, g, s] for s in range(TOPK)]
         kc = jnp.concatenate([kv_bufs[g][0][b] for b in blocks], axis=0)
-        scores = SCALE * lax.dot_general(kc, qb, NT, preferred_element_type=F32)
+        vc = jnp.concatenate([kv_bufs[g][1][b] for b in blocks], axis=0)
+        lines = jnp.concatenate([kc, vc], axis=1)
+        products = jnp.concatenate(
+            [
+                lax.dot_general(lines[:HALF_K], pair, NT, preferred_element_type=F32),
+                lax.dot_general(lines[HALF_K:], pair, NT, preferred_element_type=F32),
+            ],
+            axis=0,
+        )
+        grad_w = products[:, HD:]
         scores = jnp.concatenate(
             [
                 jnp.where(
                     base <= (own - blocks[s]) * BLOCK,
-                    scores[s * BLOCK : (s + 1) * BLOCK],
+                    products[s * BLOCK : (s + 1) * BLOCK, :HD],
                     -1e30,
                 )
                 for s in range(TOPK)
@@ -208,43 +231,38 @@
             axis=0,
         )
         top = jnp.max(scores, axis=0, keepdims=True)
-        weights = jnp.exp(scores - top)
+        weights = jnp.exp2((scores - top) * EXP2_SCALE)
         weights = weights * (1.0 / jnp.sum(weights, axis=0, keepdims=True))
         low = weights.astype(BF16)
-        vc = jnp.concatenate([kv_bufs[g][1][b] for b in blocks], axis=0)
-        grad_w = lax.dot_general(vc, gb, NT, preferred_element_type=F32)
         deltas = jnp.sum(low.astype(F32) * grad_w, axis=0, keepdims=True)
         grad_s = (weights * (grad_w - deltas)).astype(BF16)
         grad_q = SCALE * lax.dot_general(grad_s, kc, TN, preferred_element_type=F32)
         for i in range(2):
             gq_ref[rows, pl.ds((2 * g + i) * HD, HD)] = grad_q[i * BLOCK : (i + 1) * BLOCK].astype(BF16)
+        lines = jnp.concatenate([grad_s, low], axis=1)
+        term = jnp.concatenate(
+            [
+                jnp.dot(lines[:HALF_K], pair, preferred_element_type=F32),
+                jnp.dot(lines[HALF_K:], pair, preferred_element_type=F32),
+            ],
+            axis=0,
+        )
         for s in range(TOPK):
-            gs_ref[g, q, s] = grad_s[s * BLOCK : (s + 1) * BLOCK]
-            wt_ref[g, q, s] = low[s * BLOCK : (s + 1) * BLOCK]
-
-    for g in range(2):
-        for q in range(CHUNK):
-            gs_ref[g, q, TOPK] = jnp.zeros((BLOCK, HD), BF16)
-            wt_ref[g, q, TOPK] = jnp.zeros((BLOCK, HD), BF16)
+            part = term[s * BLOCK : (s + 1) * BLOCK]
+            tm_ref[q, s, :, :HD] = (SCALE * part[:, :HD]).astype(BF16)
+            tm_ref[q, s, :, HD:] = part[:, HD:].astype(BF16)
 
     def terms(g, plane):
         def body(i, carry):
-            for kv, (src, rhs) in enumerate(((gs_ref, qb_ref), (wt_ref, gb_ref))):
-                right = jnp.concatenate([rhs[g, q] for q in range(CHUNK)], axis=0)
-                lines = []
-                for b in range(2 * CHUNK):
-                    j = (plane * 4 + i) * (2 * CHUNK) + b
-                    lines.append(
-                        jnp.concatenate(
-                            [src[g, q, inv_ref[q, g, j]] for q in range(CHUNK)], axis=1
-                        )
-                    )
-                out = jnp.dot(jnp.concatenate(lines, axis=0), right, preferred_element_type=F32)
-                if kv == 0:
-                    out = SCALE * out
-                out = out.astype(BF16)
-                t_ref[2 * g + kv, plane, 0, i] = out[:ROWS]
-                t_ref[2 * g + kv, plane, 1, i] = out[ROWS:]
+            for b in range(2 * CHUNK):
+                j = (plane * 4 + i) * (2 * CHUNK) + b
+                total = tm_ref[0, inv_ref[0, g, j]].astype(F32)
+                for q in range(1, CHUNK):
+                    total = total + tm_ref[q, inv_ref[q, g, j]].astype(F32)
+                total = total.astype(BF16)
+                lines = pl.ds((b % CHUNK) * BLOCK, BLOCK)
+                t_ref[2 * g, plane, b // CHUNK, i, lines, :] = total[:, :HD]
+                t_ref[2 * g + 1, plane, b // CHUNK, i, lines, :] = total[:, HD:]
             return carry
 
         lax.fori_loop(0, 4, body, 0)
@@ -348,10 +366,9 @@
         core_sums[2 * g + 1, n].start()
 
     hooks = {
-        (0, 1): lambda: (each(gather_far, (2, 0), (3, 0)), each(gather_relay, (2, 1), (3, 1))),
-        (0, 3): lambda: each(gather_far, (2, 1), (3, 1)),
-        (1, 1): lambda: each(core_sum, (0, 0), (1, 0), (0, 1), (1, 1)),
-        (1, 3): lambda: do((0, 1), "go_far", "cross"),
+        (0, 1): lambda: each(gather_relay, (2, 1), (3, 1)),
+        (0, 2): lambda: each(gather_far, (2, 1), (3, 1)),
+        (1, 2): lambda: each(core_sum, (0, 0), (1, 0), (0, 1), (1, 1)),
     }
     for g in range(2):
         if g == 1:
@@ -370,9 +387,7 @@
         for n in range(2):
             terms(g, planes[n])
             core_start(g, n)
-            if g == 1 and n == 0:
-                do((0, 1), "relay")
-    each(core_sum, (2, 0), (3, 0))
+    do((0, 1), "go_far")
 
     for copy in weight_copies:
         copy.wait()
@@ -382,13 +397,14 @@
         acc_ref[rows, :] = lax.dot_general(wq_ref[rows, :], gq_ref[...], NT, preferred_element_type=F32)
         return carry
 
-    lax.fori_loop(0, 3, query_part, 0)
+    lax.fori_loop(0, 1, query_part, 0)
+    each(core_sum, (2, 0), (3, 0))
+    do((0, 1), "cross")
     each(core_sum, (2, 1), (3, 1))
-    lax.fori_loop(3, 6, query_part, 0)
-    do((2, 3), "go_far")
-    do((2, 3), "cross")
-    lax.fori_loop(6, 8, query_part, 0)
-    do((2, 3), "relay")
+    lax.fori_loop(1, 4, query_part, 0)
+    do((0, 1), "relay")
+    lax.fori_loop(4, 8, query_part, 0)
+    do((2, 3), "go_far", "cross", "relay")
     each(sum_end, (0,), (1,), (2,), (3,))
     out_copies.append(local(gk_ref, gk_hbm))
     out_copies.append(local(gv_ref, gv_hbm))
@@ -424,12 +440,10 @@
     both(lambda t: t.theirs_right.start())
     term_chunk(1 - yl, zl)
     both(lambda t: t.theirs_left.start())
+    term_chunk(yl, zo)
     term_chunk(yl, zl)
-    z_sums[0].direct.start()
     term_chunk(yl, zr)
-    z_sums[1].direct.start()
-    term_chunk(yl, zo)
-    both(lambda t: t.go_far())
+    both(lambda t: (t.go_far(), t.start_mine()))
     term_chunk(1 - yl, z)
     term_chunk(yl, z)
     both(lambda t: t.cross())
@@ -452,9 +466,6 @@
 
 
 def body(queries, keys, values, grad_out, chosen, w_query, w_key, w_value):
-    slots = jnp.arange(TOPK, dtype=jnp.int32)[None, None, :, None]
-    names = jnp.arange(64, dtype=jnp.int32)[None, None, None, :]
-    inverse = jnp.min(jnp.where(chosen[..., None] == names, slots, TOPK), axis=2)
     vmem = pl.BlockSpec(memory_space=pltpu.VMEM)
     smem = pl.BlockSpec(memory_space=pltpu.SMEM)
     hbm = pl.BlockSpec(memory_space=pl.ANY)
@@ -470,13 +481,13 @@
             shape((ROWS, 256), BF16),
             shape((OUT_W, ROWS), BF16),
         ),
-        in_specs=[hbm, hbm, hbm, hbm, smem, smem, hbm, hbm, hbm],
+        in_specs=[hbm, hbm, hbm, hbm, smem, vmem, hbm, hbm, hbm],
         out_specs=(hbm,) * 4,
         scratch_shapes=[
             buf(64, BLOCK, HD), buf(64, BLOCK, HD), buf(64, BLOCK, HD), buf(64, BLOCK, HD),
             buf(ROWS, 512), buf(ROWS, 512), buf(ROWS, 512), buf(ROWS, 256), buf(ROWS, 256), buf(OUT_W, ROWS),
-            buf(2, CHUNK, TOPK + 1, BLOCK, HD), buf(2, CHUNK, TOPK + 1, BLOCK, HD),
-            buf(2, CHUNK, HD, HD), buf(2, CHUNK, HD, HD),
+            buf(CHUNK, TOPK + 1, BLOCK, 2 * HD),
+            pltpu.VMEM((CHUNK, 2, HD), jnp.int32), pltpu.SMEM((CHUNK, 2, HD), jnp.int32),
             buf(4, 2, 2, 4, *chunk), buf(4, 2, 4, *chunk), buf(4, 2, 4, *chunk),
             buf(4, *chunk), buf(4, *chunk), buf(4, 2, *chunk), buf(4, 2, *chunk), buf(4, *chunk), buf(4, *chunk),
             buf(4608, 512), buf(4608, 256), buf(4608, 256), pltpu.VMEM((4608, ROWS), F32),
@@ -489,7 +500,7 @@
         compiler_params=pltpu.CompilerParams(
             collective_id=0, has_side_effects=True, vmem_limit_bytes=60 * 1024 * 1024
         ),
-    )(queries, grad_out, keys, values, chosen, inverse, w_query, w_key, w_value)
+    )(queries, grad_out, keys, values, chosen, chosen, w_query, w_key, w_value)
     grad_queries, grad_keys, grad_values, grad_input = pl.pallas_call(
         write_out,
         out_shape=tuple(shape(o.shape, o.dtype) for o in outs),

time: 83.3 us -> 75.6 us (0.908)
  Pallas kernels: 80.8 us -> 74.7 us
  other arithmetic: 1.38 us -> 0 us
    pallas_call x1, Pallas kernels: 78.7 us -> 72.6 us  [body(): pl.pallas_call(kernel, out_shape=(shape((ROWS, 512), BF16), shape((ROWS,...]
    reduce_min x1 -> x0, other arithmetic: 1.38 us -> none  [body(): jnp.min(jnp.where(chosen[..., None] == names, slots, TOPK), axis=2)]
where the time goes in v3:
time: 75.6 us; the launch traced here: 75.3 us
  Pallas kernels  74.7 us (99%)
    pallas_call x1, Pallas kernels, body(): pl.pallas_call(kernel, out_shape=(shape((ROWS, 512), BF16), shape((ROWS,...  72.6 us
    pallas_call x1, Pallas kernels, body(): pl.pallas_call(write_out, out_shape=tuple((shape(o.shape, o.dtype) for o...  2.07 us

profile of v3, /device:TPU:0, one launch (start us, length us, event | category | flops | bytes accessed | tf_op | source)
XLA Modules:
  0.0 75.3 jit_solution(6410301019782289149)
XLA Ops:
  0.6 72.6 %shard_map.111 = (bf16[256,512]{1,0:T(8,128)(2,1)}, bf16[256,256]{1,0:T(8,128)(2,1)}, bf16[256,256]{1,0:T(8,128)(2,1)}, bf16[576,256]{1,0:T(8,128)(2,1)}) custom-call(bf16[256,512]{1,0:T(8,128)(2,1)} %q_hbm.1, bf16[256,512]{1,0:T(8,128)(2,1)} %go_hbm.1, bf16[256,256]{1,0:T(8,128)(2,1)} %k_hbm.1, bf16[256,256]{1,0:T(8,128)(2,1)} %v_hbm.1, ...), custom_call_target="tpu_custom_call" | custom-call | tf_op jit(solution)/shard_map/pallas_call | solution.py:476
  73.2 2.1 %shard_map.112 = (bf16[256,512]{1,0:T(8,128)(2,1)}, bf16[256,256]{1,0:T(8,128)(2,1)}, bf16[256,256]{1,0:T(8,128)(2,1)}, bf16[576,256]{1,0:T(8,128)(2,1)}) custom-call(bf16[256,512]{1,0:T(8,128)(2,1)} %get-tuple-element.12.refs_0_, bf16[256,256]{1,0:T(8,128)(2,1)} %get-tuple-element.13.refs_1_, bf16[256,256]{1,0:T(8,128)(2,1)} %get-tuple-element.14.refs_2_, ...), custom_call_target="tpu_custom_call" | custom-call | tf_op jit(solution)/shard_map/pallas_call | solution.py:504

commit v4 on v3

--- a/solution.py
+++ b/solution.py
@@ -23,7 +23,7 @@
 TN = (((0,), (0,)), ((), ()))
 F32 = jnp.float32
 BF16 = jnp.bfloat16
-N_COPIES = 144
+N_COPIES = 184
 
 
 def kernel(
@@ -293,10 +293,16 @@
             self.relay_at = right if way == 0 else left
             self.over = plan(stage, last, over)
 
-        def start_theirs(self):
+        def start_first(self):
             self.first.start()
+
+        def start_near(self):
             self.theirs_right.start()
             self.theirs_left.start()
+
+        def start_theirs(self):
+            self.start_first()
+            self.start_near()
 
         def start_mine(self):
             self.direct.start()
@@ -330,45 +336,51 @@
             self.over.wait_recv()
             return total + last[...].astype(F32)
 
-    x_sums = [
-        Sum(
-            u % 2, s_ref.at[u, py], s_ref.at[u, yh],
-            (xa_ref.at[u], xf_ref.at[u], xl_ref.at[u, 0], xr_ref.at[u, 0],
-             xl_ref.at[u, 1], xr_ref.at[u, 1], xs_ref.at[u], xy_ref.at[u]),
+    x_sums = {
+        (u, e): Sum(
+            u % 2, s_ref.at[u, e, py], s_ref.at[u, e, yh],
+            (xa_ref.at[u, e], xf_ref.at[u, e], xl_ref.at[u, e, 0], xr_ref.at[u, e, 0],
+             xl_ref.at[u, e, 1], xr_ref.at[u, e, 1], xs_ref.at[u, e], xy_ref.at[u, e]),
             (x, xr, xl, xo), (to_right, to_left), to_y,
         )
         for u in range(4)
-    ]
+        for e in range(2)
+    }
 
     def core_sum(u, n):
         plane = planes[n]
         core_sums[u, n].wait_recv()
-        for xx in range(4):
-            s_ref[u, plane, xx] = (
-                t_ref[u, plane, k, xx].astype(F32) + p_ref[u, plane, xx].astype(F32)
-            ).astype(BF16)
-        if n == 0:
-            x_sums[u].start_theirs()
-        else:
-            x_sums[u].start_mine()
-
-    def sum_end(u):
+        for e in range(2):
+            half = pl.ds(e * HD, HD)
+            for xx in range(4):
+                s_ref[u, e, plane, xx] = (
+                    t_ref[u, plane, k, xx, half, :].astype(F32) + p_ref[u, plane, xx, half, :].astype(F32)
+                ).astype(BF16)
+
+    def sum_end(u, e):
         g, kv = units[u]
-        (gk_ref, gv_ref)[kv][:, pl.ds(g * HD, HD)] = x_sums[u].end().astype(BF16)
+        (gk_ref, gv_ref)[kv][pl.ds(e * HD, HD), pl.ds(g * HD, HD)] = x_sums[u, e].end().astype(BF16)
 
     def do(names, *steps):
         for step in steps:
-            for u in names:
-                getattr(x_sums[u], step)()
+            for name in names:
+                getattr(x_sums[name], step)()
 
     def core_start(g, n):
         core_sums[2 * g, n].start()
         core_sums[2 * g + 1, n].start()
 
+    LOW = [[(0, e), (1, e)] for e in range(2)]
+    HIGH = [[(2, e), (3, e)] for e in range(2)]
     hooks = {
         (0, 1): lambda: each(gather_relay, (2, 1), (3, 1)),
         (0, 2): lambda: each(gather_far, (2, 1), (3, 1)),
-        (1, 2): lambda: each(core_sum, (0, 0), (1, 0), (0, 1), (1, 1)),
+        (1, 2): lambda: (
+            each(core_sum, (0, 0), (1, 0)),
+            do(LOW[0] + LOW[1], "start_theirs"),
+            each(core_sum, (0, 1), (1, 1)),
+            do(LOW[0] + LOW[1], "start_mine"),
+        ),
     }
     for g in range(2):
         if g == 1:
@@ -387,7 +399,7 @@
         for n in range(2):
             terms(g, planes[n])
             core_start(g, n)
-    do((0, 1), "go_far")
+    do(LOW[0] + LOW[1], "go_far")
 
     for copy in weight_copies:
         copy.wait()
@@ -397,62 +409,90 @@
         acc_ref[rows, :] = lax.dot_general(wq_ref[rows, :], gq_ref[...], NT, preferred_element_type=F32)
         return carry
 
-    lax.fori_loop(0, 1, query_part, 0)
     each(core_sum, (2, 0), (3, 0))
-    do((0, 1), "cross")
+    do(HIGH[0], "start_theirs")
+    do(HIGH[1], "start_first")
     each(core_sum, (2, 1), (3, 1))
-    lax.fori_loop(1, 4, query_part, 0)
-    do((0, 1), "relay")
-    lax.fori_loop(4, 8, query_part, 0)
-    do((2, 3), "go_far", "cross", "relay")
-    each(sum_end, (0,), (1,), (2,), (3,))
+    do(LOW[0], "cross")
+    lax.fori_loop(0, 4, query_part, 0)
+    do(LOW[0] + LOW[1], "relay")
+    lax.fori_loop(4, 5, query_part, 0)
+    do(HIGH[0], "go_far", "start_mine", "cross")
+    do(LOW[1], "cross")
+    do(HIGH[1][:1], "start_near")
+    lax.fori_loop(5, 8, query_part, 0)
+    do(HIGH[0], "relay")
+    do(HIGH[1][1:], "start_near")
+    do(HIGH[1], "go_far", "start_mine")
+    each(sum_end, *((u, 0) for u in range(4)))
+
+    z_places = (z, zr, zl, zo)
+    z_sums = {
+        (e, w): Sum(
+            w, pt_ref.at[e, w, 1 - yl], pt_ref.at[e, w, yl],
+            (za_ref.at[e, w], zf_ref.at[e, w], zl_ref.at[e, w, 0], zr_ref.at[e, w, 0],
+             zl_ref.at[e, w, 1], zr_ref.at[e, w, 1], zs_ref.at[e, w], zy_ref.at[e, w]),
+            z_places, (to_zr, to_zl), to_yl,
+        )
+        for e in range(2)
+        for w in range(2)
+    }
+
+    def term_chunk(e, side, zz):
+        i = zz * 2 + side
+        rows = pl.ds(pl.multiple_of(i * OUT_W, OUT_W), OUT_W)
+        half = pl.ds(e * HD, HD)
+        out = acc_ref[rows, half]
+        out = out + lax.dot_general(wk_ref[rows, :], gk_ref[half, :], NT, preferred_element_type=F32)
+        out = out + lax.dot_general(wv_ref[rows, :], gv_ref[half, :], NT, preferred_element_type=F32)
+        out = out.astype(BF16)
+        for w in range(2):
+            pt_ref[e, w, side, zz] = out[w * HALF_W : (w + 1) * HALF_W]
+
+    def both(e, step):
+        for w in range(2):
+            step(z_sums[e, w])
+
+    def send_theirs(e):
+        term_chunk(e, 1 - yl, zo)
+        both(e, lambda t: t.first.start())
+        term_chunk(e, 1 - yl, zr)
+        both(e, lambda t: t.theirs_right.start())
+        term_chunk(e, 1 - yl, zl)
+        both(e, lambda t: t.theirs_left.start())
+
+    def own_chunks(e):
+        for zz in (zo, zl, zr):
+            term_chunk(e, yl, zz)
+
+    def last_chunks(e):
+        term_chunk(e, 1 - yl, z)
+        term_chunk(e, yl, z)
+
+    def z_end(e):
+        for w in range(2):
+            gi_ref[pl.ds(w * HALF_W, HALF_W), pl.ds(e * HD, HD)] = z_sums[e, w].end().astype(BF16)
+
+    send_theirs(0)
+    do(HIGH[1], "cross")
+    own_chunks(0)
+    do(HIGH[1], "relay")
+    last_chunks(0)
+    both(0, lambda t: (t.go_far(), t.start_mine()))
+    each(sum_end, *((u, 1) for u in range(4)))
     out_copies.append(local(gk_ref, gk_hbm))
     out_copies.append(local(gv_ref, gv_hbm))
-
-    z_places = (z, zr, zl, zo)
-    z_sums = [
-        Sum(
-            w, pt_ref.at[w, 1 - yl], pt_ref.at[w, yl],
-            (za_ref.at[w], zf_ref.at[w], zl_ref.at[w, 0], zr_ref.at[w, 0],
-             zl_ref.at[w, 1], zr_ref.at[w, 1], zs_ref.at[w], zy_ref.at[w]),
-            z_places, (to_zr, to_zl), to_yl,
-        )
-        for w in range(2)
-    ]
-
-    def term_chunk(side, zz):
-        i = zz * 2 + side
-        rows = pl.ds(pl.multiple_of(i * OUT_W, OUT_W), OUT_W)
-        out = acc_ref[rows, :]
-        out = out + lax.dot_general(wk_ref[rows, :], gk_ref[...], NT, preferred_element_type=F32)
-        out = out + lax.dot_general(wv_ref[rows, :], gv_ref[...], NT, preferred_element_type=F32)
-        out = out.astype(BF16)
-        for w in range(2):
-            pt_ref[w, side, zz] = out[w * HALF_W : (w + 1) * HALF_W]
-
-    def both(step):
-        for w in range(2):
-            step(z_sums[w])
-
-    term_chunk(1 - yl, zo)
-    both(lambda t: t.first.start())
-    term_chunk(1 - yl, zr)
-    both(lambda t: t.theirs_right.start())
-    term_chunk(1 - yl, zl)
-    both(lambda t: t.theirs_left.start())
-    term_chunk(yl, zo)
-    term_chunk(yl, zl)
-    term_chunk(yl, zr)
-    both(lambda t: (t.go_far(), t.start_mine()))
-    term_chunk(1 - yl, z)
-    term_chunk(yl, z)
-    both(lambda t: t.cross())
-    both(lambda t: t.relay())
-    for w in range(2):
-        gi_ref[pl.ds(w * HALF_W, HALF_W), :] = z_sums[w].end().astype(BF16)
-        out_copies.append(
-            local(gi_ref.at[pl.ds(w * HALF_W, HALF_W)], gi_hbm.at[pl.ds(w * HALF_W, HALF_W)])
-        )
+    send_theirs(1)
+    own_chunks(1)
+    last_chunks(1)
+    both(0, lambda t: t.cross())
+    both(1, lambda t: (t.go_far(), t.start_mine()))
+    both(0, lambda t: t.relay())
+    both(1, lambda t: t.cross())
+    both(1, lambda t: t.relay())
+    z_end(0)
+    z_end(1)
+    out_copies.append(local(gi_ref, gi_hbm))
 
     for copy in out_copies:
         copy.wait()
@@ -472,7 +512,7 @@
     shape = jax.ShapeDtypeStruct
     buf = lambda *dims: pltpu.VMEM(dims, BF16)
     chunk = (ROWS, HD)
-    zc = (HALF_W, ROWS)
+    zc = (2, HALF_W, HD)
     outs = pl.pallas_call(
         kernel,
         out_shape=(
@@ -488,11 +528,11 @@
             buf(ROWS, 512), buf(ROWS, 512), buf(ROWS, 512), buf(ROWS, 256), buf(ROWS, 256), buf(OUT_W, ROWS),
             buf(CHUNK, TOPK + 1, BLOCK, 2 * HD),
             pltpu.VMEM((CHUNK, 2, HD), jnp.int32), pltpu.SMEM((CHUNK, 2, HD), jnp.int32),
-            buf(4, 2, 2, 4, *chunk), buf(4, 2, 4, *chunk), buf(4, 2, 4, *chunk),
-            buf(4, *chunk), buf(4, *chunk), buf(4, 2, *chunk), buf(4, 2, *chunk), buf(4, *chunk), buf(4, *chunk),
+            buf(4, 2, 2, 4, *chunk), buf(4, 2, 4, *chunk), buf(4, 2, 2, 4, HD, HD),
+            buf(4, 2, HD, HD), buf(4, 2, HD, HD), buf(4, 2, 2, HD, HD), buf(4, 2, 2, HD, HD), buf(4, 2, HD, HD), buf(4, 2, HD, HD),
             buf(4608, 512), buf(4608, 256), buf(4608, 256), pltpu.VMEM((4608, ROWS), F32),
-            buf(2, 2, 4, *zc), buf(2, *zc), buf(2, *zc),
-            buf(2, 2, *zc), buf(2, 2, *zc), buf(2, *zc), buf(2, *zc),
+            buf(2, 2, 2, 4, HALF_W, HD), buf(2, *zc), buf(2, *zc),
+            buf(2, 2, 2, HALF_W, HD), buf(2, 2, 2, HALF_W, HD), buf(2, *zc), buf(2, *zc),
             pltpu.SemaphoreType.DMA((N_COPIES,)),
             pltpu.SemaphoreType.DMA((N_COPIES,)),
             pltpu.SemaphoreType.DMA((32,)),

time: 75.6 us -> 73.7 us (0.975)
  Pallas kernels: 74.7 us -> 72.9 us
    pallas_call x1, Pallas kernels: 72.6 us -> 70.9 us  [body(): pl.pallas_call(kernel, out_shape=(shape((ROWS, 512), BF16), shape((ROWS,...]
where the time goes in v4:
time: 73.7 us; the launch traced here: 73.6 us
  Pallas kernels  72.9 us (99%)
    pallas_call x1, Pallas kernels, body(): pl.pallas_call(kernel, out_shape=(shape((ROWS, 512), BF16), shape((ROWS,...  70.9 us
    pallas_call x1, Pallas kernels, body(): pl.pallas_call(write_out, out_shape=tuple((shape(o.shape, o.dtype) for o...  2.07 us

profile of v4, /device:TPU:0, one launch (start us, length us, event | category | flops | bytes accessed | tf_op | source)
XLA Modules:
  0.0 73.6 jit_solution(2283846098988115524)
XLA Ops:
  0.6 70.9 %shard_map.111 = (bf16[256,512]{1,0:T(8,128)(2,1)}, bf16[256,256]{1,0:T(8,128)(2,1)}, bf16[256,256]{1,0:T(8,128)(2,1)}, bf16[576,256]{1,0:T(8,128)(2,1)}) custom-call(bf16[256,512]{1,0:T(8,128)(2,1)} %q_hbm.1, bf16[256,512]{1,0:T(8,128)(2,1)} %go_hbm.1, bf16[256,256]{1,0:T(8,128)(2,1)} %k_hbm.1, bf16[256,256]{1,0:T(8,128)(2,1)} %v_hbm.1, ...), custom_call_target="tpu_custom_call" | custom-call | tf_op jit(solution)/shard_map/pallas_call | solution.py:516
  71.5 2.1 %shard_map.112 = (bf16[256,512]{1,0:T(8,128)(2,1)}, bf16[256,256]{1,0:T(8,128)(2,1)}, bf16[256,256]{1,0:T(8,128)(2,1)}, bf16[576,256]{1,0:T(8,128)(2,1)}) custom-call(bf16[256,512]{1,0:T(8,128)(2,1)} %get-tuple-element.12.refs_0_, bf16[256,256]{1,0:T(8,128)(2,1)} %get-tuple-element.13.refs_1_, bf16[256,256]{1,0:T(8,128)(2,1)} %get-tuple-element.14.refs_2_, ...), custom_call_target="tpu_custom_call" | custom-call | tf_op jit(solution)/shard_map/pallas_call | solution.py:544

commit v5 on v4

--- a/solution.py
+++ b/solution.py
@@ -27,10 +27,10 @@
 
 
 def kernel(
-    q_hbm, go_hbm, k_hbm, v_hbm, ch_ref, chv_ref, wq_hbm, wk_hbm, wv_hbm,
+    q_hbm, go_hbm, k_hbm, v_hbm, ch_hbm, wq_hbm, wk_hbm, wv_hbm,
     gq_hbm, gk_hbm, gv_hbm, gi_hbm,
     kv00, kv01, kv10, kv11, q_ref, go_ref, gq_ref, gk_ref, gv_ref, gi_ref,
-    tm_ref, names_ref, inv_ref,
+    tm_ref, ch_ref, chv_ref, names_ref, inv_ref,
     t_ref, p_ref, s_ref, xa_ref, xf_ref, xl_ref, xr_ref, xs_ref, xy_ref,
     wq_ref, wk_ref, wv_ref, acc_ref, pt_ref, za_ref, zf_ref, zl_ref, zr_ref, zs_ref, zy_ref,
     send_sem, recv_sem, local_sem,
@@ -81,6 +81,12 @@
         pl.semaphore_signal(barrier, inc=1, device_id=where, device_id_type=pl.DeviceIdType.MESH)
 
     own_copies = []
+    choice_copies = [
+        pltpu.make_async_copy(ch_hbm, chv_ref, local_sem.at[30]),
+        pltpu.make_async_copy(ch_hbm, ch_ref, local_sem.at[31]),
+    ]
+    for copy in choice_copies:
+        copy.start()
     n_local = 0
     for g in range(2):
         for kv in range(2):
@@ -108,6 +114,8 @@
     weight_copies = [local(wq_hbm, wq_ref), local(wk_hbm, wk_ref), local(wv_hbm, wv_ref)]
     out_copies = []
 
+    for copy in choice_copies:
+        copy.wait()
     lanes = lax.broadcasted_iota(jnp.int32, (2, HD), 1)
     for q in range(CHUNK):
         picked = chv_ref[q]
@@ -373,9 +381,11 @@
     LOW = [[(0, e), (1, e)] for e in range(2)]
     HIGH = [[(2, e), (3, e)] for e in range(2)]
     hooks = {
-        (0, 1): lambda: each(gather_relay, (2, 1), (3, 1)),
-        (0, 2): lambda: each(gather_far, (2, 1), (3, 1)),
-        (1, 2): lambda: (
+        (0, 1): lambda: (
+            each(gather_relay, (2, 1), (3, 1)),
+            each(gather_far, (2, 1), (3, 1)),
+        ),
+        (1, 1): lambda: (
             each(core_sum, (0, 0), (1, 0)),
             do(LOW[0] + LOW[1], "start_theirs"),
             each(core_sum, (0, 1), (1, 1)),
@@ -390,10 +400,11 @@
             for (gg, at), action in hooks.items():
                 if gg == g:
                     pl.when(q == at)(lambda action=action: (action(), None)[1])
-            attend(g, q)
+            attend(g, 2 * q)
+            attend(g, 2 * q + 1)
             return carry
 
-        lax.fori_loop(0, CHUNK, step, 0)
+        lax.fori_loop(0, CHUNK // 2, step, 0)
         if g == 1:
             out_copies.append(local(gq_ref, gq_hbm))
         for n in range(2):
@@ -453,9 +464,11 @@
         for w in range(2):
             step(z_sums[e, w])
 
-    def send_theirs(e):
+    def send_first(e):
         term_chunk(e, 1 - yl, zo)
         both(e, lambda t: t.first.start())
+
+    def send_near(e):
         term_chunk(e, 1 - yl, zr)
         both(e, lambda t: t.theirs_right.start())
         term_chunk(e, 1 - yl, zl)
@@ -473,16 +486,18 @@
         for w in range(2):
             gi_ref[pl.ds(w * HALF_W, HALF_W), pl.ds(e * HD, HD)] = z_sums[e, w].end().astype(BF16)
 
-    send_theirs(0)
+    send_first(0)
+    do(HIGH[1], "relay")
+    send_near(0)
     do(HIGH[1], "cross")
     own_chunks(0)
-    do(HIGH[1], "relay")
     last_chunks(0)
     both(0, lambda t: (t.go_far(), t.start_mine()))
     each(sum_end, *((u, 1) for u in range(4)))
     out_copies.append(local(gk_ref, gk_hbm))
     out_copies.append(local(gv_ref, gv_hbm))
-    send_theirs(1)
+    send_first(1)
+    send_near(1)
     own_chunks(1)
     last_chunks(1)
     both(0, lambda t: t.cross())
@@ -501,13 +516,19 @@
 
 
 def write_out(*refs):
-    for src, dst in zip(refs[:4], refs[4:]):
-        dst[...] = src[...]
+    sources, targets, held, sem = refs[:4], refs[4:8], refs[8:12], refs[12]
+    loads = [pltpu.make_async_copy(sources[i], held[i], sem.at[i]) for i in range(4)]
+    stores = [pltpu.make_async_copy(held[i], targets[i], sem.at[4 + i]) for i in range(4)]
+    for copy in loads:
+        copy.start()
+    for load, store in zip(loads, stores):
+        load.wait()
+        store.start()
+    for copy in stores:
+        copy.wait()
 
 
 def body(queries, keys, values, grad_out, chosen, w_query, w_key, w_value):
-    vmem = pl.BlockSpec(memory_space=pltpu.VMEM)
-    smem = pl.BlockSpec(memory_space=pltpu.SMEM)
     hbm = pl.BlockSpec(memory_space=pl.ANY)
     shape = jax.ShapeDtypeStruct
     buf = lambda *dims: pltpu.VMEM(dims, BF16)
@@ -521,12 +542,13 @@
             shape((ROWS, 256), BF16),
             shape((OUT_W, ROWS), BF16),
         ),
-        in_specs=[hbm, hbm, hbm, hbm, smem, vmem, hbm, hbm, hbm],
+        in_specs=[hbm] * 8,
         out_specs=(hbm,) * 4,
         scratch_shapes=[
             buf(64, BLOCK, HD), buf(64, BLOCK, HD), buf(64, BLOCK, HD), buf(64, BLOCK, HD),
             buf(ROWS, 512), buf(ROWS, 512), buf(ROWS, 512), buf(ROWS, 256), buf(ROWS, 256), buf(OUT_W, ROWS),
             buf(CHUNK, TOPK + 1, BLOCK, 2 * HD),
+            pltpu.SMEM((CHUNK, 2, TOPK), jnp.int32), pltpu.VMEM((CHUNK, 2, TOPK), jnp.int32),
             pltpu.VMEM((CHUNK, 2, HD), jnp.int32), pltpu.SMEM((CHUNK, 2, HD), jnp.int32),
             buf(4, 2, 2, 4, *chunk), buf(4, 2, 4, *chunk), buf(4, 2, 2, 4, HD, HD),
             buf(4, 2, HD, HD), buf(4, 2, HD, HD), buf(4, 2, 2, HD, HD), buf(4, 2, 2, HD, HD), buf(4, 2, HD, HD), buf(4, 2, HD, HD),
@@ -540,12 +562,14 @@
         compiler_params=pltpu.CompilerParams(
             collective_id=0, has_side_effects=True, vmem_limit_bytes=60 * 1024 * 1024
         ),
-    )(queries, grad_out, keys, values, chosen, chosen, w_query, w_key, w_value)
+    )(queries, grad_out, keys, values, chosen, w_query, w_key, w_value)
     grad_queries, grad_keys, grad_values, grad_input = pl.pallas_call(
         write_out,
         out_shape=tuple(shape(o.shape, o.dtype) for o in outs),
-        in_specs=[vmem] * 4,
-        out_specs=(vmem,) * 4,
+        in_specs=[hbm] * 4,
+        out_specs=(hbm,) * 4,
+        scratch_shapes=[pltpu.VMEM(o.shape, o.dtype) for o in outs] + [pltpu.SemaphoreType.DMA((8,))],
+        compiler_params=pltpu.CompilerParams(vmem_limit_bytes=60 * 1024 * 1024),
     )(*outs)
     return grad_queries, grad_keys, grad_values, grad_input.T
 

time: 73.7 us -> 72.4 us (0.982)
  Pallas kernels: 72.9 us -> 71.6 us
    pallas_call x1, Pallas kernels: 70.9 us -> 69.6 us  [body(): pl.pallas_call(kernel, out_shape=(shape((ROWS, 512), BF16), shape((ROWS,...]
where the time goes in v5:
time: 72.4 us; the launch traced here: 72.2 us
  Pallas kernels  71.6 us (99%)
    pallas_call x1, Pallas kernels, body(): pl.pallas_call(kernel, out_shape=(shape((ROWS, 512), BF16), shape((ROWS,...  69.6 us
    pallas_call x1, Pallas kernels, body(): pl.pallas_call(write_out, out_shape=tuple((shape(o.shape, o.dtype) for o...  1.95 us

profile of v5, /device:TPU:0, one launch (start us, length us, event | category | flops | bytes accessed | tf_op | source)
XLA Modules:
  0.0 72.2 jit_solution(3522333948723004827)
XLA Ops:
  0.6 69.6 %shard_map.111 = (bf16[256,512]{1,0:T(8,128)(2,1)}, bf16[256,256]{1,0:T(8,128)(2,1)}, bf16[256,256]{1,0:T(8,128)(2,1)}, bf16[576,256]{1,0:T(8,128)(2,1)}) custom-call(bf16[256,512]{1,0:T(8,128)(2,1)} %q_hbm.1, bf16[256,512]{1,0:T(8,128)(2,1)} %go_hbm.1, bf16[256,256]{1,0:T(8,128)(2,1)} %k_hbm.1, bf16[256,256]{1,0:T(8,128)(2,1)} %v_hbm.1, ...), custom_call_target="tpu_custom_call" | custom-call | tf_op jit(solution)/shard_map/pallas_call | solution.py:537
  70.2 2.0 %shard_map.112 = (bf16[256,512]{1,0:T(8,128)(2,1)}, bf16[256,256]{1,0:T(8,128)(2,1)}, bf16[256,256]{1,0:T(8,128)(2,1)}, bf16[576,256]{1,0:T(8,128)(2,1)}) custom-call(bf16[256,512]{1,0:T(8,128)(2,1)} %get-tuple-element.12.refs_0_, bf16[256,256]{1,0:T(8,128)(2,1)} %get-tuple-element.13.refs_1_, bf16[256,256]{1,0:T(8,128)(2,1)} %get-tuple-element.14.refs_2_, ...), custom_call_target="tpu_custom_call" | custom-call | tf_op jit(solution)/shard_map/pallas_call | solution.py:566

commit v6 on v5

--- a/solution.py
+++ b/solution.py
@@ -56,6 +56,7 @@
     to_yl = (c, z * 2 + (1 - yl))
 
     started = []
+    one_way = set()
 
     def plan(src, dst, where):
         i = len(started)
@@ -283,7 +284,9 @@
     }
 
     class Sum:
-        def __init__(self, way, theirs, mine, bufs, places, ends, over):
+        def __init__(self, way, theirs, mine, bufs, places, ends, over, sender=None):
+            self.sender = sender
+            begin = len(started)
             self.way, self.theirs, self.mine, self.bufs = way, theirs, mine, bufs
             self.here, right, left, across = places
             self.across = across
@@ -292,6 +295,9 @@
             self.first = plan(theirs.at[across], first, over)
             self.theirs_right = plan(theirs.at[right], l1, go_right)
             self.theirs_left = plan(theirs.at[left], r1, go_left)
+            self.over = plan(stage, last, over)
+            if sender is not None:
+                one_way.update(range(begin, len(started)))
             self.far = plan(mine.at[across], far, go_right if way == 0 else go_left)
             self.mine_right = plan(mine.at[right], l0, go_right)
             self.mine_left = plan(mine.at[left], r0, go_left)
@@ -299,14 +305,22 @@
                 (self.mine_right, self.mine_left) if way == 0 else (self.mine_left, self.mine_right)
             )
             self.relay_at = right if way == 0 else left
-            self.over = plan(stage, last, over)
+
+        def gate(self, sends, action):
+            if self.sender is None:
+                action()
+            else:
+                pl.when(self.sender if sends else jnp.logical_not(self.sender))(action)
 
         def start_first(self):
-            self.first.start()
+            self.gate(True, self.first.start)
 
         def start_near(self):
-            self.theirs_right.start()
-            self.theirs_left.start()
+            def action():
+                self.theirs_right.start()
+                self.theirs_left.start()
+
+            self.gate(True, action)
 
         def start_theirs(self):
             self.start_first()
@@ -318,18 +332,27 @@
         def add(self, i, buf):
             self.mine[i] = (self.mine[i].astype(F32) + buf[...].astype(F32)).astype(BF16)
 
+        def far_now(self):
+            self.gate(True, self.far.start)
+
         def go_far(self):
-            self.first.wait_recv()
-            self.add(self.across, self.bufs[0])
-            self.far.start()
+            def action():
+                self.first.wait_recv()
+                self.add(self.across, self.bufs[0])
+                self.far.start()
+
+            self.gate(False, action)
 
         def cross(self):
-            _, _, _, _, l1, r1, stage, _ = self.bufs
-            self.theirs_right.wait_recv()
-            self.theirs_left.wait_recv()
-            total = self.theirs[self.here].astype(F32) + l1[...].astype(F32) + r1[...].astype(F32)
-            stage[...] = total.astype(BF16)
-            self.over.start()
+            def action():
+                _, _, _, _, l1, r1, stage, _ = self.bufs
+                self.theirs_right.wait_recv()
+                self.theirs_left.wait_recv()
+                total = self.theirs[self.here].astype(F32) + l1[...].astype(F32) + r1[...].astype(F32)
+                stage[...] = total.astype(BF16)
+                self.over.start()
+
+            self.gate(True, action)
 
         def relay(self):
             self.far.wait_recv()
@@ -341,15 +364,21 @@
             self.mine_right.wait_recv()
             self.mine_left.wait_recv()
             total = self.mine[self.here].astype(F32) + l0[...].astype(F32) + r0[...].astype(F32)
-            self.over.wait_recv()
+            self.gate(False, self.over.wait_recv)
             return total + last[...].astype(F32)
+
+    later = yh == 1
+
+    @pl.when(later)
+    def _():
+        xy_ref[...] = jnp.zeros(xy_ref.shape, BF16)
 
     x_sums = {
         (u, e): Sum(
             u % 2, s_ref.at[u, e, py], s_ref.at[u, e, yh],
             (xa_ref.at[u, e], xf_ref.at[u, e], xl_ref.at[u, e, 0], xr_ref.at[u, e, 0],
              xl_ref.at[u, e, 1], xr_ref.at[u, e, 1], xs_ref.at[u, e], xy_ref.at[u, e]),
-            (x, xr, xl, xo), (to_right, to_left), to_y,
+            (x, xr, xl, xo), (to_right, to_left), to_y, later,
         )
         for u in range(4)
         for e in range(2)
@@ -389,7 +418,7 @@
             each(core_sum, (0, 0), (1, 0)),
             do(LOW[0] + LOW[1], "start_theirs"),
             each(core_sum, (0, 1), (1, 1)),
-            do(LOW[0] + LOW[1], "start_mine"),
+            do(LOW[0] + LOW[1], "far_now", "start_mine"),
         ),
     }
     for g in range(2):
@@ -424,17 +453,19 @@
     do(HIGH[0], "start_theirs")
     do(HIGH[1], "start_first")
     each(core_sum, (2, 1), (3, 1))
+    do(HIGH[0], "far_now")
     do(LOW[0], "cross")
     lax.fori_loop(0, 4, query_part, 0)
+    do(HIGH[0], "go_far")
     do(LOW[0] + LOW[1], "relay")
     lax.fori_loop(4, 5, query_part, 0)
-    do(HIGH[0], "go_far", "start_mine", "cross")
+    do(HIGH[0], "start_mine", "cross")
     do(LOW[1], "cross")
     do(HIGH[1][:1], "start_near")
     lax.fori_loop(5, 8, query_part, 0)
     do(HIGH[0], "relay")
     do(HIGH[1][1:], "start_near")
-    do(HIGH[1], "go_far", "start_mine")
+    do(HIGH[1], "far_now", "go_far", "start_mine")
     each(sum_end, *((u, 0) for u in range(4)))
 
     z_places = (z, zr, zl, zo)
@@ -486,10 +517,10 @@
         for w in range(2):
             gi_ref[pl.ds(w * HALF_W, HALF_W), pl.ds(e * HD, HD)] = z_sums[e, w].end().astype(BF16)
 
+    do(HIGH[1], "cross")
     send_first(0)
     do(HIGH[1], "relay")
     send_near(0)
-    do(HIGH[1], "cross")
     own_chunks(0)
     last_chunks(0)
     both(0, lambda t: (t.go_far(), t.start_mine()))
@@ -511,8 +542,11 @@
 
     for copy in out_copies:
         copy.wait()
-    for copy in started:
-        copy.wait_send()
+    for i, copy in enumerate(started):
+        if i in one_way:
+            pl.when(later)(copy.wait_send)
+        else:
+            copy.wait_send()
 
 
 def write_out(*refs):

time: 72.4 us -> 71.1 us (0.982)
  Pallas kernels: 71.6 us -> 70.1 us
    pallas_call x1, Pallas kernels: 69.6 us -> 68.1 us  [body(): pl.pallas_call(kernel, out_shape=(shape((ROWS, 512), BF16), shape((ROWS,...]
where the time goes in v6:
time: 71.1 us; the launch traced here: 70.7 us
  Pallas kernels  70.1 us (99%)
    pallas_call x1, Pallas kernels, body(): pl.pallas_call(kernel, out_shape=(shape((ROWS, 512), BF16), shape((ROWS,...  68.1 us
    pallas_call x1, Pallas kernels, body(): pl.pallas_call(write_out, out_shape=tuple((shape(o.shape, o.dtype) for o...  1.95 us

profile of v6, /device:TPU:0, one launch (start us, length us, event | category | flops | bytes accessed | tf_op | source)
XLA Modules:
  0.0 70.7 jit_solution(1617153008119891256)
XLA Ops:
  0.6 68.1 %shard_map.111 = (bf16[256,512]{1,0:T(8,128)(2,1)}, bf16[256,256]{1,0:T(8,128)(2,1)}, bf16[256,256]{1,0:T(8,128)(2,1)}, bf16[576,256]{1,0:T(8,128)(2,1)}) custom-call(bf16[256,512]{1,0:T(8,128)(2,1)} %q_hbm.1, bf16[256,512]{1,0:T(8,128)(2,1)} %go_hbm.1, bf16[256,256]{1,0:T(8,128)(2,1)} %k_hbm.1, bf16[256,256]{1,0:T(8,128)(2,1)} %v_hbm.1, ...), custom_call_target="tpu_custom_call" | custom-call | tf_op jit(solution)/shard_map/pallas_call | solution.py:571
  68.7 2.0 %shard_map.112 = (bf16[256,512]{1,0:T(8,128)(2,1)}, bf16[256,256]{1,0:T(8,128)(2,1)}, bf16[256,256]{1,0:T(8,128)(2,1)}, bf16[576,256]{1,0:T(8,128)(2,1)}) custom-call(bf16[256,512]{1,0:T(8,128)(2,1)} %get-tuple-element.12.refs_0_, bf16[256,256]{1,0:T(8,128)(2,1)} %get-tuple-element.13.refs_1_, bf16[256,256]{1,0:T(8,128)(2,1)} %get-tuple-element.14.refs_2_, ...), custom_call_target="tpu_custom_call" | custom-call | tf_op jit(solution)/shard_map/pallas_call | solution.py:600

commit v7 on v6

--- a/solution.py
+++ b/solution.py
@@ -515,7 +515,9 @@
 
     def z_end(e):
         for w in range(2):
-            gi_ref[pl.ds(w * HALF_W, HALF_W), pl.ds(e * HD, HD)] = z_sums[e, w].end().astype(BF16)
+            part = (pl.ds(w * HALF_W, HALF_W), pl.ds(e * HD, HD))
+            gi_ref[part] = z_sums[e, w].end().astype(BF16)
+            out_copies.append(local(gi_ref.at[part], gi_hbm.at[part]))
 
     do(HIGH[1], "cross")
     send_first(0)
@@ -538,7 +540,6 @@
     both(1, lambda t: t.relay())
     z_end(0)
     z_end(1)
-    out_copies.append(local(gi_ref, gi_hbm))
 
     for copy in out_copies:
         copy.wait()

time: 71.1 us -> 71 us (level)
  no operation moved by 1% of the time
where the time goes in v7:
time: 71 us; the launch traced here: 70.7 us
  Pallas kernels  70 us (99%)
    pallas_call x1, Pallas kernels, body(): pl.pallas_call(kernel, out_shape=(shape((ROWS, 512), BF16), shape((ROWS,...  68.1 us
    pallas_call x1, Pallas kernels, body(): pl.pallas_call(write_out, out_shape=tuple((shape(o.shape, o.dtype) for o...  1.95 us

profile of v7, /device:TPU:0, one launch (start us, length us, event | category | flops | bytes accessed | tf_op | source)
XLA Modules:
  0.0 70.7 jit_solution(10460254279676012129)
XLA Ops:
  0.6 68.1 %shard_map.111 = (bf16[256,512]{1,0:T(8,128)(2,1)}, bf16[256,256]{1,0:T(8,128)(2,1)}, bf16[256,256]{1,0:T(8,128)(2,1)}, bf16[576,256]{1,0:T(8,128)(2,1)}) custom-call(bf16[256,512]{1,0:T(8,128)(2,1)} %q_hbm.1, bf16[256,512]{1,0:T(8,128)(2,1)} %go_hbm.1, bf16[256,256]{1,0:T(8,128)(2,1)} %k_hbm.1, bf16[256,256]{1,0:T(8,128)(2,1)} %v_hbm.1, ...), custom_call_target="tpu_custom_call" | custom-call | tf_op jit(solution)/shard_map/pallas_call | solution.py:572
  68.7 2.0 %shard_map.112 = (bf16[256,512]{1,0:T(8,128)(2,1)}, bf16[256,256]{1,0:T(8,128)(2,1)}, bf16[256,256]{1,0:T(8,128)(2,1)}, bf16[576,256]{1,0:T(8,128)(2,1)}) custom-call(bf16[256,512]{1,0:T(8,128)(2,1)} %get-tuple-element.12.refs_0_, bf16[256,256]{1,0:T(8,128)(2,1)} %get-tuple-element.13.refs_1_, bf16[256,256]{1,0:T(8,128)(2,1)} %get-tuple-element.14.refs_2_, ...), custom_call_target="tpu_custom_call" | custom-call | tf_op jit(solution)/shard_map/pallas_call | solution.py:601
